TPU v7x, 512 devices: a whole 4x4x16 slice. The times are simulated.
512 devices in a mesh: hist: 16 (over z), rows: 32 (over x, y, core).
Axes of the slice: x: 4, y: 4, z: 16, core: 2. Of those that a mesh axis runs over, the one named last changes fastest.
Arguments:
- g_hist: bfloat16 [352, 64, 352, 128], P('hist', None, 'rows'), may hold values from -0.0390625 to 0.0390625
- g_last: float32 [64, 352, 128], P(None, 'rows'), may hold values from -6 to 6
- integral_last: float32 [64, 352, 128], P(None, 'rows'), may hold values from -6 to 6
- coupling: float32 [64, 64], replicated, may hold values from 0.5 to 2
- step_re: float32 [64, 64], replicated, may hold values from -1 to 2
- step_im: float32 [64, 64], replicated, may hold values from -0.375 to 0.375
Outputs:
- new_row: float32 [64, 352, 128], P('hist', 'rows')
- new_integral: float32 [64, 352, 128], P('hist', 'rows')
All inputs are finite; a program needn't handle non-finite values.
Results may differ from a plain program's by a relative error of at most 0.0055.
Values may be sent and summed in bfloat16 or wider, within the bound.
No kernel may reach another device: no remote copies, remote signals or barrier semaphores. Data moves between devices by JAX's collectives and lax.ppermute only.
A program may use at most 64 MiB of HBM per device.

v0:
```python
import functools

import jax
import jax.numpy as jnp
from jax import lax
from jax.sharding import Mesh
from jax.sharding import PartitionSpec as P

ITERS = 3
ROWS = ("rows_0", "rows_1", "rows_2")
HIST_ROWS = ("hist", "rows_0", "rows_1", "rows_2")


step_size = 0.5
half_step = 0.25


def over_axes(shard, axes):
    return functools.reduce(lax.psum, axes, shard)


def picked(shard, axis, root):
    return lax.dynamic_index_in_dim(lax.all_gather(shard, axis), root, 0, keepdims=False)


def split_up(shard, dim, peers):
    before, after = (shard.shape[:dim], shard.shape[dim + 1 :])
    return jnp.moveaxis(shard.reshape(*before, peers, -1, *after), dim, 0)


def summed_on_arrival(shard, axis, dim):
    parts = split_up(shard, dim, lax.axis_size(axis))
    arrived = lax.all_to_all(parts, axis, split_axis=0, concat_axis=0, tiled=True)
    return arrived.sum(axis=0)


def combine(first, second, width):
    return jnp.concatenate(
        [first[..., :width] - second[..., width:], first[..., width:] + second[..., :width]], -1
    )


def apply_step(step_re, step_im, field):
    orbits, times, wide = field.shape
    flat = field.reshape(orbits, times * wide)
    first = jnp.dot(
        step_re, flat, precision=lax.Precision.HIGHEST, preferred_element_type=jnp.float32
    ).reshape(orbits, times, wide)
    second = jnp.dot(
        step_im, flat, precision=lax.Precision.HIGHEST, preferred_element_type=jnp.float32
    ).reshape(orbits, times, wide)
    return combine(first, second, orbits)


def diag_power(field, offset):
    count, times, wide = field.shape
    orbits = wide // 2
    mask = (jnp.arange(count)[:, None] + offset == jnp.arange(orbits)[None, :]).astype(jnp.float32)
    real_part = field[..., :orbits]
    imag_part = field[..., orbits:]
    return jnp.sum((real_part * real_part + imag_part * imag_part) * mask[:, None, :])


def time_weights(first_time, count):
    moments = first_time + jnp.arange(count)
    return step_size * jnp.where(moments == 0, 0.5, 1.0).astype(jnp.float32)


def sigma_of(field, coupling, scale, weights):
    orbits = field.shape[0]
    real_part = field[..., :orbits]
    imag_part = field[..., orbits:]
    factor = (
        coupling[:, None, :]
        * (real_part * real_part + imag_part * imag_part)
        / scale
        * weights[None, :, None]
    )
    return jnp.concatenate([factor * real_part, factor * imag_part], -1).astype(jnp.bfloat16)


def on_device(g_hist, g_last, integral_last, coupling, step_re, step_im):
    orbits = g_last.shape[0]
    row_count = g_last.shape[1]
    wide = 2 * orbits
    hist_size = lax.axis_size("hist")
    rows_size = lax.axis_size(ROWS)
    fan_out = rows_size // hist_size
    hist_at = lax.axis_index("hist")
    total_cells = row_count * rows_size * orbits
    share = orbits // hist_size
    shifted = jnp.concatenate(
        [
            g_last[..., :orbits] + half_step * integral_last[..., orbits:],
            g_last[..., orbits:] - half_step * integral_last[..., :orbits],
        ],
        -1,
    )
    base = apply_step(step_re, step_im, shifted)
    base_part = lax.dynamic_slice_in_dim(base, hist_at * share, share, 0)
    history = g_hist.reshape(g_hist.shape[0] * orbits, row_count * wide)
    field = g_last
    part = lax.dynamic_slice_in_dim(g_last, hist_at * share, share, 0)
    integral_part = part
    for iteration in range(ITERS):
        power = over_axes(diag_power(part, hist_at * share), HIST_ROWS)
        if iteration > 0:
            field = lax.all_gather(part, "hist", axis=0, tiled=True)
        scale = 1.0 + power / total_cells
        accumulated = jnp.zeros((wide, row_count * wide), jnp.float32)
        for member in range(fan_out):
            root = fan_out * hist_at + member
            remote = picked(field, ROWS, root)
            sigma_block = sigma_of(
                remote, coupling, scale, time_weights(root * row_count, row_count)
            )
            left_side = jnp.concatenate(
                [
                    sigma_block[..., :orbits].reshape(orbits, row_count * orbits),
                    sigma_block[..., orbits:].reshape(orbits, row_count * orbits),
                ],
                0,
            )
            block = lax.slice_in_dim(
                history, member * row_count * orbits, (member + 1) * row_count * orbits, axis=0
            )
            accumulated = accumulated + jnp.dot(
                left_side, block, preferred_element_type=jnp.float32
            )
        product = accumulated.reshape(wide, row_count, wide)
        terms = combine(product[:orbits], product[orbits:], orbits)
        integral_part = summed_on_arrival(terms, "hist", 0)
        part = base_part + jnp.concatenate(
            [half_step * integral_part[..., orbits:], -half_step * integral_part[..., :orbits]], -1
        )
    return (part, integral_part)


def solution(mesh):
    split = Mesh(
        mesh.devices.reshape(mesh.shape["hist"], 4, 4, 2), ("hist", "rows_0", "rows_1", "rows_2")
    )
    return jax.shard_map(
        on_device,
        mesh=split,
        in_specs=(
            P("hist", None, ROWS, None),
            P(None, ROWS, None),
            P(None, ROWS, None),
            P(),
            P(),
            P(),
        ),
        out_specs=(P("hist", ROWS, None), P("hist", ROWS, None)),
        check_vma=False,
    )
```

profile of v0, /device:TPU:4, one launch (start us, length us, event | category | flops | bytes accessed | tf_op | source)
XLA Modules:
  0.0 447.4 jit_solution(11925732724214413689)
XLA Ops:
  7.2 0.7 all-gather.7.cloned.1.call-update
  8.0 1.6 fusion.46
  9.6 37.1 %psum.84 = f32[]{:T(128)} all-reduce(f32[]{:T(128)} %fusion.46), channel_id=1, replica_groups=mesh['hist'=16,'rows_0'=4,'rows_1'=4,'rows_2'=2] {'hist'}, use_global_device_ids=true, to_apply=%region_1.0 | all-reduce | flops 1 | bytes 8 | tf_op jit(solution)/shard_map/psum | solution.py:19
  46.7 8.9 %psum.85 = f32[]{:T(128)} all-reduce(f32[]{:T(128)} %psum.84), channel_id=1, replica_groups=mesh['hist'=16,'rows_0'=4,'rows_1'=4,'rows_2'=2] {'rows_0'}, use_global_device_ids=true, to_apply=%region_2.0 | all-reduce | flops 1 | bytes 8 | tf_op jit(solution)/shard_map/psum | solution.py:19
  55.6 11.3 %psum.86 = f32[]{:T(128)} all-reduce(f32[]{:T(128)} %psum.85), channel_id=1, replica_groups=mesh['hist'=16,'rows_0'=4,'rows_1'=4,'rows_2'=2] {'rows_1'}, use_global_device_ids=true, to_apply=%region_3.0 | all-reduce | flops 1 | bytes 8 | tf_op jit(solution)/shard_map/psum | solution.py:19
  67.0 3.1 psum.87
  70.0 0.8 copy.48
  70.9 3.2 fusion.57
  74.0 3.2 copy.52
  77.3 1.6 copy.50
  79.5 11.7 %all-gather.7.cloned.1.call-done = f32[2048,11,128]{2,0,1:T(8,128)} async-done(((f32[64,11,128]{2,0,1:T(8,128)}), f32[2048,11,128]{2,0,1:T(8,128)}) %all-gather.7.cloned.1.call-update) | async-done | bytes 11534352 | tf_op jit(solution)/shard_map/all_gather | solution.py:23
  91.2 1.9 constant_dynamic-slice_fusion.4
  93.1 2.1 copy.51
  95.2 1.1 copy.49
  96.4 1.7 multiply_convert_fusion.9
  99.4 0.9 fusion.60
  100.3 1.0 slice.243
  101.4 1.8 slice.246
  103.2 1.5 slice_subtract_fusion.2
  105.0 0.9 copy.53
  105.8 12.4 %all-to-all-start = ((f32[16,4,11,128]{3,1,2,0:T(4,128)}), f32[16,4,11,128]{3,1,2,0:T(4,128)}, u32[]{:S(2)}, u32[]{:S(2)}) async-start(f32[16,4,11,128]{3,1,2,0:T(4,128)} %copy.53), calls=%async_computation | async-start | bytes 720896 | tf_op jit(solution)/shard_map/all_to_all | solution.py:33
  118.3 1.3 multiply_add_fusion
  119.6 0.7 copy-done.6
  120.5 1.3 convolution_bitcast_fusion.1
  121.8 1.0 reshape.109
  122.8 2.4 convolution_bitcast_fusion
  125.2 1.8 reshape.110
  127.1 1.4 fusion.62
  128.7 1.1 copy_add_fusion
  129.8 11.6 %all-to-all-done = f32[16,4,11,128]{3,1,2,0:T(4,128)} async-done(((f32[16,4,11,128]{3,1,2,0:T(4,128)}), f32[16,4,11,128]{3,1,2,0:T(4,128)}, u32[]{:S(2)}, u32[]{:S(2)}) %all-to-all-start) | async-done | bytes 360480 | tf_op jit(solution)/shard_map/all_to_all | solution.py:33
  141.4 1.1 reduce_sum.55
  142.5 0.9 maximum_add_fusion
  143.4 32.8 %all_gather.32 = f32[64,11,128]{2,1,0:T(8,128)S(1)} all-gather(f32[4,11,128]{2,1,0:T(8,128)S(1)} %copy.54), channel_id=1, replica_groups=mesh['hist'=16,'rows_0'=4,'rows_1'=4,'rows_2'=2] {'hist'}, dimensions={0}, use_global_device_ids=true | all-gather | bytes 382976 | tf_op jit(solution)/shard_map/all_gather | solution.py:108
  176.3 0.8 copy.55
  177.2 0.7 fusion.43
  177.9 27.6 %psum.88 = f32[]{:T(128)} all-reduce(f32[]{:T(128)} %fusion.43), channel_id=1, replica_groups=mesh['hist'=16,'rows_0'=4,'rows_1'=4,'rows_2'=2] {'hist'}, use_global_device_ids=true, to_apply=%region_7.8 | all-reduce | flops 1 | bytes 8 | tf_op jit(solution)/shard_map/psum | solution.py:19
  205.5 8.9 %psum.89 = f32[]{:T(128)} all-reduce(f32[]{:T(128)} %psum.88), channel_id=1, replica_groups=mesh['hist'=16,'rows_0'=4,'rows_1'=4,'rows_2'=2] {'rows_0'}, use_global_device_ids=true, to_apply=%region_8.9 | all-reduce | flops 1 | bytes 8 | tf_op jit(solution)/shard_map/psum | solution.py:19
  214.4 9.4 %psum.90 = f32[]{:T(128)} all-reduce(f32[]{:T(128)} %psum.89), channel_id=1, replica_groups=mesh['hist'=16,'rows_0'=4,'rows_1'=4,'rows_2'=2] {'rows_1'}, use_global_device_ids=true, to_apply=%region_9.10 | all-reduce | flops 1 | bytes 8 | tf_op jit(solution)/shard_map/psum | solution.py:19
  223.8 3.3 psum.91
  227.7 17.3 %all-gather.9.cloned.1.call-done = f32[2048,11,128]{2,0,1:T(8,128)} async-done(((f32[64,11,128]{2,0,1:T(8,128)}), f32[2048,11,128]{2,0,1:T(8,128)}) %all-gather.9.cloned.1.call-update) | async-done | bytes 11534352 | tf_op jit(solution)/shard_map/all_gather | solution.py:23
  245.0 1.9 constant_dynamic-slice_fusion.2
  246.9 2.1 copy.57
  249.0 1.1 copy.56
  250.1 1.7 multiply_convert_fusion.5
  251.8 0.7 fusion.5
  253.2 0.9 fusion.59
  254.1 1.0 slice.263
  255.1 1.8 slice.266
  257.0 1.5 slice_subtract_fusion.1
  258.9 35.1 %all_to_all.15 = f32[16,4,11,128]{3,1,2,0:T(4,128)S(1)} all-to-all(f32[16,4,11,128]{3,1,2,0:T(4,128)S(1)} %copy.58), channel_id=1, replica_groups=mesh['hist'=16,'rows_0'=4,'rows_1'=4,'rows_2'=2] {'hist'}, dimensions={0} | all-to-all | bytes 720896 | tf_op jit(solution)/shard_map/all_to_all | solution.py:33
  294.2 32.9 %all_gather.35 = f32[64,11,128]{2,1,0:T(8,128)S(1)} all-gather(f32[4,11,128]{2,1,0:T(8,128)S(1)} %copy.59), channel_id=1, replica_groups=mesh['hist'=16,'rows_0'=4,'rows_1'=4,'rows_2'=2] {'hist'}, dimensions={0}, use_global_device_ids=true | all-gather | bytes 382976 | tf_op jit(solution)/shard_map/all_gather | solution.py:108
  327.1 0.8 copy.60
  328.0 0.7 fusion.40
  328.6 27.6 %psum.92 = f32[]{:T(128)} all-reduce(f32[]{:T(128)} %fusion.40), channel_id=1, replica_groups=mesh['hist'=16,'rows_0'=4,'rows_1'=4,'rows_2'=2] {'hist'}, use_global_device_ids=true, to_apply=%region_13.14 | all-reduce | flops 1 | bytes 8 | tf_op jit(solution)/shard_map/psum | solution.py:19
  356.3 8.5 %psum.93 = f32[]{:T(128)} all-reduce(f32[]{:T(128)} %psum.92), channel_id=1, replica_groups=mesh['hist'=16,'rows_0'=4,'rows_1'=4,'rows_2'=2] {'rows_0'}, use_global_device_ids=true, to_apply=%region_14.15 | all-reduce | flops 1 | bytes 8 | tf_op jit(solution)/shard_map/psum | solution.py:19
  364.8 9.8 %psum.94 = f32[]{:T(128)} all-reduce(f32[]{:T(128)} %psum.93), channel_id=1, replica_groups=mesh['hist'=16,'rows_0'=4,'rows_1'=4,'rows_2'=2] {'rows_1'}, use_global_device_ids=true, to_apply=%region_15.16 | all-reduce | flops 1 | bytes 8 | tf_op jit(solution)/shard_map/psum | solution.py:19
  374.6 3.1 psum.95
  378.3 17.5 %all-gather.11.cloned.1.call-done = f32[2048,11,128]{2,0,1:T(8,128)} async-done(((f32[64,11,128]{2,0,1:T(8,128)}), f32[2048,11,128]{2,0,1:T(8,128)}) %all-gather.11.cloned.1.call-update) | async-done | bytes 11534352 | tf_op jit(solution)/shard_map/all_gather | solution.py:23
  395.8 1.9 constant_dynamic-slice_fusion
  397.6 2.1 copy.62
  399.8 1.1 copy.61
  400.9 1.7 multiply_convert_fusion.1
  404.8 35.2 %all_to_all.16 = f32[16,4,11,128]{3,1,2,0:T(4,128)S(1)} all-to-all(f32[16,4,11,128]{3,1,2,0:T(4,128)S(1)} %copy.63), channel_id=1, replica_groups=mesh['hist'=16,'rows_0'=4,'rows_1'=4,'rows_2'=2] {'hist'}, dimensions={0} | all-to-all | bytes 720896 | tf_op jit(solution)/shard_map/all_to_all | solution.py:33
  440.1 0.7 maximum_add_fusion.2
  (51 shorter events, 5.7 us)
Async XLA Ops:
  7.2 113.3 %copy-start = (f32[64,64]{1,0:T(8,128)S(1)}, f32[64,64]{1,0:T(8,128)}, u32[]{:S(2)}) copy-start(f32[64,64]{1,0:T(8,128)} %param.10) | copy-start | bytes 49156
  7.2 84.1 %all-gather.7.cloned.1.call-start = ((), (), s32[]{:S(2)}) async-start(), calls=%async_computation.3 | async-start | bytes 11894784 | tf_op jit(solution)/shard_map/all_gather | solution.py:23
  96.4 2.4 copy-start.2
  104.7 13.5 %copy-start.5 = (f32[64,11,128]{2,0,1:T(8,128)S(1)}, f32[64,11,128]{2,0,1:T(8,128)}, u32[]{:S(2)}) copy-start(f32[64,11,128]{2,0,1:T(8,128)} %param.7) | copy-start | bytes 1081348
  105.0 17.9 %copy-start.9 = (f32[64,64]{1,0:T(8,128)S(1)}, f32[64,64]{1,0:T(8,128)}, u32[]{:S(2)}) copy-start(f32[64,64]{1,0:T(8,128)} %param.11) | copy-start | bytes 49156
  105.8 35.6 %all-to-all-start = ((f32[16,4,11,128]{3,1,2,0:T(4,128)}), f32[16,4,11,128]{3,1,2,0:T(4,128)}, u32[]{:S(2)}, u32[]{:S(2)}) async-start(f32[16,4,11,128]{3,1,2,0:T(4,128)} %copy.53), calls=%async_computation | async-start | bytes 720896 | tf_op jit(solution)/shard_map/all_to_all | solution.py:33
  118.2 126.8 %all-gather.9.cloned.1.call-start = ((), (), s32[]{:S(2)}) async-start(), calls=%async_computation.4 | async-start | bytes 11894784 | tf_op jit(solution)/shard_map/all_gather | solution.py:23
  119.6 0.8 copy-start.6
  119.6 0.8 copy-start.7
  177.2 218.6 %all-gather.11.cloned.1.call-start = ((), (), s32[]{:S(2)}) async-start(), calls=%async_computation.5 | async-start | bytes 11894784 | tf_op jit(solution)/shard_map/all_gather | solution.py:23
  250.1 2.4 copy-start.3
  400.9 2.4 copy-start.4
  404.1 36.8 %copy-start.1 = (f32[64,64]{1,0:T(8,128)S(1)}, f32[64,64]{1,0:T(8,128)}, u32[]{:S(2)}) copy-start(f32[64,64]{1,0:T(8,128)} %param.10) | copy-start | bytes 49156
  440.1 0.8 copy-start.8
Sparse Core Ops, SparseCore 0:
  11.2 79.9 all-gather.6
  177.3 67.6 all-gather.8
  328.1 67.6 all-gather.10
where the time goes:
time: 449 us; the launch traced here: 447 us
  blocking collectives  295 us (66%)
  waiting for transfers between devices  58.8 us (13%)
  local copies, waits for them, and re-layouts  40.2 us (9%)
  other arithmetic  17.8 us (4%)
  between operations  16 us (4%)
  starting transfers between devices  12.5 us (3%)
  matrix products  7.54 us (2%)
    psum x12, blocking collectives, over_axes(): return functools.reduce(lax.psum, axes, shard)  159 us
    all_to_all x2, blocking collectives, summed_on_arrival(): lax.all_to_all(parts, axis, split_axis=0, concat_axis=0, tiled=True)  70.3 us
    all_gather x2, blocking collectives, on_device(): field = lax.all_gather(part, 'hist', axis=0, tiled=True)  65.7 us
    all_gather x3, waiting for transfers between devices, picked(): lax.all_gather(shard, axis)  46.5 us
    dynamic_slice x9, local copies, waits for them, and re-layouts, picked(): lax.dynamic_index_in_dim(lax.all_gather(shard, axis), root, 0, keepdims=F...  15.4 us
    all_to_all x1, starting transfers between devices, summed_on_arrival(): lax.all_to_all(parts, axis, split_axis=0, concat_axis=0, tiled=True)  12.4 us
    all_to_all x1, waiting for transfers between devices, summed_on_arrival(): lax.all_to_all(parts, axis, split_axis=0, concat_axis=0, tiled=True)  11.6 us
  transfers between devices with their start and end apart: 4, of which 4 were waited for; matrix products, arithmetic and copies ran while one was open for 5% of the time, Pallas kernels for 0%

commit v1 on v0

v1 whole, which is shorter than its diff:
```python
import jax
import jax.numpy as jnp
from jax import lax
from jax.sharding import Mesh
from jax.sharding import PartitionSpec as P

ITERS = 3
ROWS = ("rows_0", "rows_1", "rows_2")
EVERY = ("hist", "rows_0", "rows_1", "rows_2")
SMALL = 2.0**-90
LARGE = 2.0**90

step_size = 0.5
half_step = 0.25


def narrow(value):
    return lax.reduce_precision(value, 8, 7)


def rows_of(values, wide):
    return jnp.stack([jnp.broadcast_to(value, (wide,)) for value in values]).astype(jnp.bfloat16)


def halves(value):
    high = narrow(value)
    return high, narrow(value - high)


def on_device(g_hist, g_last, integral_last, coupling, step_re, step_im):
    orbits = g_last.shape[0]
    row_count = g_last.shape[1]
    wide = 2 * orbits
    hist_size = lax.axis_size("hist")
    rows_size = lax.axis_size(ROWS)
    fan_out = rows_size // hist_size
    hist_at = lax.axis_index("hist")
    rows_at = lax.axis_index(ROWS)
    total_cells = row_count * rows_size * orbits
    share = orbits // hist_size
    cells = share * row_count
    padded = -(-(cells + 3) // 16) * 16
    swap = [
        ((z * hist_size + p) * fan_out + k, (p * hist_size + z) * fan_out + k)
        for z in range(hist_size)
        for p in range(hist_size)
        for k in range(fan_out)
    ]

    def my_rows(whole):
        return lax.dynamic_slice_in_dim(whole, hist_at * share, share, 0)

    def fill(rows):
        return jnp.zeros((*rows, padded - cells - 3, wide), jnp.bfloat16)

    part = my_rows(g_last)
    coupling_part = my_rows(coupling)
    moments = rows_at * row_count + jnp.arange(row_count)
    weights = step_size * jnp.where(moments == 0, 0.5, 1.0).astype(jnp.float32)
    factors = coupling_part[:, None, :] * weights[None, :, None]
    mask = (jnp.arange(share)[:, None] + hist_at * share == jnp.arange(orbits)[None, :]).astype(
        jnp.float32
    )

    def piece_of(part, damping):
        real_part = part[..., :orbits]
        imag_part = part[..., orbits:]
        square = real_part * real_part + imag_part * imag_part
        power = jnp.sum(square * mask[:, None, :])
        peak = jnp.max(square)
        factor = factors * (square * damping)
        sigma = jnp.concatenate([factor * real_part, factor * imag_part], -1)
        sigma = sigma.astype(jnp.bfloat16).reshape(cells, wide)
        return jnp.concatenate([sigma, rows_of((*halves(power), peak), wide), fill(())], 0)

    shifted = jnp.concatenate(
        [
            g_last[..., :orbits] + half_step * integral_last[..., orbits:],
            g_last[..., orbits:] - half_step * integral_last[..., :orbits],
        ],
        -1,
    )
    steps = jnp.concatenate([my_rows(step_re), my_rows(step_im)], 0)
    moved = jnp.dot(
        steps,
        shifted.reshape(orbits, row_count * wide),
        precision=lax.Precision.HIGHEST,
        preferred_element_type=jnp.float32,
    ).reshape(2, share, row_count, wide)
    base_part = jnp.concatenate(
        [
            moved[0, ..., :orbits] - moved[1, ..., orbits:],
            moved[0, ..., orbits:] + moved[1, ..., :orbits],
        ],
        -1,
    )
    history = g_hist.reshape(g_hist.shape[0] * orbits, row_count * wide)
    damping, restore = jnp.float32(1.0), jnp.float32(1.0)
    integral_part = part
    for iteration in range(ITERS):
        piece = lax.ppermute(piece_of(part, damping), EVERY, swap)
        copies = jnp.broadcast_to(piece[None], (rows_size, padded, wide))
        pieces = lax.all_to_all(copies, ROWS, split_axis=0, concat_axis=0, tiled=True)
        marks = pieces[:, cells : cells + 3, 0].astype(jnp.float32)
        power = jnp.sum(marks[:, :2])
        peak = jnp.max(marks[:, 2])
        sigma = pieces[:, :cells].reshape(hist_size, fan_out, share, row_count, 2, orbits)
        left = sigma.transpose(4, 0, 2, 1, 3, 5).reshape(wide, fan_out * row_count * orbits)
        product = jnp.dot(left, history, preferred_element_type=jnp.float32)
        product = product.reshape(2, orbits, row_count, wide)
        terms = jnp.concatenate(
            [
                product[0, ..., :orbits] - product[1, ..., orbits:],
                product[0, ..., orbits:] + product[1, ..., :orbits],
            ],
            -1,
        ).astype(jnp.bfloat16)
        terms = terms.reshape(hist_size, cells, wide)
        notes = jnp.broadcast_to(rows_of((*halves(power), peak), wide), (hist_size, 3, wide))
        sent = jnp.concatenate([terms, notes, fill((hist_size,))], 1)
        arrived = lax.all_to_all(sent, "hist", split_axis=0, concat_axis=0, tiled=True)
        marks = arrived[:, cells : cells + 3, 0].astype(jnp.float32)
        scale = 1.0 + jnp.sum(marks[:, :2]) / total_cells
        total = jnp.sum(arrived[:, :cells].astype(jnp.float32), 0)
        integral_part = (total / scale * restore).reshape(share, row_count, wide)
        part = base_part + jnp.concatenate(
            [half_step * integral_part[..., orbits:], -half_step * integral_part[..., :orbits]], -1
        )
        if iteration == 1:
            far = jnp.max(marks[:, 2]) > 2.0**13
            damping = jnp.where(far, SMALL, 1.0)
            restore = jnp.where(far, LARGE, 1.0)
    return (part, integral_part)


def solution(mesh):
    split = Mesh(
        mesh.devices.reshape(mesh.shape["hist"], 4, 4, 2), ("hist", "rows_0", "rows_1", "rows_2")
    )
    return jax.shard_map(
        on_device,
        mesh=split,
        in_specs=(
            P("hist", None, ROWS, None),
            P(None, ROWS, None),
            P(None, ROWS, None),
            P(),
            P(),
            P(),
        ),
        out_specs=(P("hist", ROWS, None), P("hist", ROWS, None)),
        check_vma=False,
    )
```

time: 449 us -> 246 us (0.55)
  the two profiles are of different devices: /device:TPU:4 before, /device:TPU:32 now
where the time goes in v1:
time: 246 us; the launch traced here: 245 us
  blocking collectives  72.5 us (29%)
  starting transfers between devices  44.5 us (18%)
  waiting for transfers between devices  44 us (18%)
  local copies, waits for them, and re-layouts  28.9 us (12%)
  between operations  25.6 us (10%)
  other arithmetic  18.7 us (8%)
  matrix products  10.6 us (4%)
    all_to_all x2, blocking collectives, on_device(): lax.all_to_all(copies, ROWS, split_axis=0, concat_axis=0, tiled=True)  51 us
    all_to_all x2, waiting for transfers between devices, on_device(): lax.all_to_all(sent, 'hist', split_axis=0, concat_axis=0, tiled=True)  32.2 us
    all_to_all x1, blocking collectives, on_device(): lax.all_to_all(sent, 'hist', split_axis=0, concat_axis=0, tiled=True)  21.5 us
    all_to_all x2, starting transfers between devices, on_device(): lax.all_to_all(sent, 'hist', split_axis=0, concat_axis=0, tiled=True)  18.9 us
    all_to_all x1, starting transfers between devices, on_device(): lax.all_to_all(copies, ROWS, split_axis=0, concat_axis=0, tiled=True)  18 us
    ppermute x3, waiting for transfers between devices, on_device(): piece = lax.ppermute(piece_of(part, damping), EVERY, swap)  11.8 us
    dot_general x3, matrix products, on_device(): product = jnp.dot(left, history, preferred_element_type=jnp.float32)  10.1 us
    unnamed x18, local copies, waits for them, and re-layouts  9.99 us
  transfers between devices with their start and end apart: 6, of which 5 were waited for; matrix products, arithmetic and copies ran while one was open for 7% of the time, Pallas kernels for 0%

profile of v1, /device:TPU:32, one launch (start us, length us, event | category | flops | bytes accessed | tf_op | source)
XLA Modules:
  0.0 244.9 jit_solution(3606308555951519684)
XLA Ops:
  0.7 1.6 fusion.20
  5.6 0.7 constant_dynamic-slice_fusion
  6.3 0.9 multiply_convert_fusion.5
  7.9 0.6 stack_broadcast_in_dim.55
  8.6 0.7 stack_broadcast_in_dim.56
  9.3 3.0 %collective-permute-start = (bf16[48,128]{1,0:T(8,128)(2,1)S(1)}, bf16[48,128]{1,0:T(8,128)(2,1)S(1)}, u32[]{:S(2)}, u32[]{:S(2)}) collective-permute-start(bf16[48,128]{1,0:T(8,128)(2,1)S(1)} %concatenate.87), channel_id=1, source_target_pairs={{0,0},{1,1},{2,32},{3,33},{4,64},{5,65},{6,96},{7,97},{8,128},{9,1... | collective-permute-start | bytes 36872 | tf_op jit(solution)/shard_map/ppermute | solution.py:101
  12.3 3.5 %collective-permute-done = bf16[48,128]{1,0:T(8,128)(2,1)S(1)} collective-permute-done((bf16[48,128]{1,0:T(8,128)(2,1)S(1)}, bf16[48,128]{1,0:T(8,128)(2,1)S(1)}, u32[]{:S(2)}, u32[]{:S(2)}) %collective-permute-start) | collective-permute-done | bytes 12320 | tf_op jit(solution)/shard_map/ppermute | solution.py:101
  15.8 0.8 broadcast_in_dim.22
  16.6 18.0 %all-to-all-start = ((bf16[32,48,128]{2,1,0:T(8,128)(2,1)}), bf16[32,48,128]{2,1,0:T(8,128)(2,1)S(1)}, u32[]{:S(2)}, u32[]{:S(2)}) async-start(bf16[32,48,128]{2,1,0:T(8,128)(2,1)} %broadcast_in_dim.22), calls=%async_computation | async-start | bytes 786432 | tf_op jit(solution)/shard_map/all_to_all | solution.py:103
  34.6 5.7 %copy.200 = bf16[22,64,11,128]{3,2,1,0:T(8,128)(2,1)S(1)} copy(bf16[22,64,11,128]{3,1,2,0:T(8,128)(2,1)} %param.6) | data formatting | bytes 7929856 | tf_op args[0]
  40.3 3.9 %copy.268 = bf16[176,8,11,128]{3,1,2,0:T(8,128)(2,1)} copy(bf16[176,8,11,128]{3,2,1,0:T(8,128)(2,1)S(1)} %bitcast.92) | data formatting | bytes 7929856
  44.2 6.2 %copy.201 = bf16[1408,1408]{1,0:T(8,128)(2,1)} copy(bf16[1408,1408]{0,1:T(8,128)(2,1)} %bitcast.93) | data formatting | bytes 7929856 | tf_op jit(solution)/shard_map/dot_general | solution.py:109
  50.6 0.6 slice_reduce_fusion.7
  51.3 0.6 slice_reduce_fusion.3
  55.1 0.3 reshape.148
  55.4 0.5 copy.199
  55.9 0.7 reshape.158
  56.6 3.4 %fusion.12 = f32[2,64,11,128]{3,1,2,0:T(8,128)S(1)} fusion(bf16[11,128,1408,1]{2,1,0,3:T(8,128)(2,1)} %bitcast.89, bf16[2,64,1408,1]{2,1,0,3:T(8,128)(2,1)S(1)} %reshape.158), kind=kOutput, calls=%fused_computation.25 | convolution fusion | flops 507510784 | bytes 5046272 | tf_op jit(solution)/shard_map/dot_general | solution.py:109
  60.0 0.3 fusion.7
  60.5 0.1 copy.202
  61.3 1.4 maximum_maximum_fusion.5
  62.7 0.8 maximum_maximum_fusion
  63.6 12.9 %all-to-all-start.1 = ((bf16[16,48,128]{2,1,0:T(8,128)(2,1)}), bf16[16,48,128]{2,1,0:T(8,128)(2,1)S(1)}, u32[]{:S(2)}, u32[]{:S(2)}) async-start(bf16[16,48,128]{2,1,0:T(8,128)(2,1)} %maximum_maximum_fusion), calls=%async_computation.1 | async-start | bytes 393216 | tf_op jit(solution)/shard_map/all_to_all | solution.py:121
  76.5 0.3 multiply_add_fusion
  76.7 0.4 fusion
  77.2 15.6 %all-to-all-done.1 = bf16[16,48,128]{2,1,0:T(8,128)(2,1)S(1)} async-done(((bf16[16,48,128]{2,1,0:T(8,128)(2,1)}), bf16[16,48,128]{2,1,0:T(8,128)(2,1)S(1)}, u32[]{:S(2)}, u32[]{:S(2)}) %all-to-all-start.1) | async-done | bytes 196640 | tf_op jit(solution)/shard_map/all_to_all | solution.py:121
  92.9 0.6 convert_reduce_fusion.4
  94.5 0.7 fusion.19
  99.0 0.6 stack_broadcast_in_dim.61
  99.7 0.7 stack_broadcast_in_dim.62
  100.4 2.7 %collective-permute-start.1 = (bf16[48,128]{1,0:T(8,128)(2,1)S(1)}, bf16[48,128]{1,0:T(8,128)(2,1)S(1)}, u32[]{:S(2)}, u32[]{:S(2)}) collective-permute-start(bf16[48,128]{1,0:T(8,128)(2,1)S(1)} %concatenate.94), channel_id=1, source_target_pairs={{0,0},{1,1},{2,32},{3,33},{4,64},{5,65},{6,96},{7,97},{8,128},{9,1... | collective-permute-start | bytes 36872 | tf_op jit(solution)/shard_map/ppermute | solution.py:101
  103.1 3.8 %collective-permute-done.1 = bf16[48,128]{1,0:T(8,128)(2,1)S(1)} collective-permute-done((bf16[48,128]{1,0:T(8,128)(2,1)S(1)}, bf16[48,128]{1,0:T(8,128)(2,1)S(1)}, u32[]{:S(2)}, u32[]{:S(2)}) %collective-permute-start.1) | collective-permute-done | bytes 12320 | tf_op jit(solution)/shard_map/ppermute | solution.py:101
  106.9 27.7 %all_to_all.30 = bf16[32,48,128]{2,1,0:T(8,128)(2,1)S(1)} all-to-all(bf16[32,48,128]{2,1,0:T(8,128)(2,1)S(1)} %broadcast_in_dim.24), channel_id=1, replica_groups=mesh['hist'=16,'rows_0'=4,'rows_1'=4,'rows_2'=2] {'rows_0','rows_1','row..., dimensions={0} | all-to-all | bytes 786432 | tf_op jit(solution)/shard_map/all_to_all | solution.py:103
  134.7 0.6 slice_reduce_fusion.6
  135.3 0.6 slice_reduce_fusion.2
  139.1 0.3 reshape.150
  139.5 0.5 copy.211
  140.0 0.7 reshape.160
  140.7 3.4 %fusion.10 = f32[2,64,11,128]{3,1,2,0:T(8,128)S(1)} fusion(bf16[11,128,1408,1]{2,1,0,3:T(8,128)(2,1)} %bitcast.90, bf16[2,64,1408,1]{2,1,0,3:T(8,128)(2,1)S(1)} %reshape.160), kind=kOutput, calls=%fused_computation.23 | convolution fusion | flops 507510784 | bytes 5046272 | tf_op jit(solution)/shard_map/dot_general | solution.py:109
  144.0 0.3 fusion.5
  145.3 1.4 maximum_maximum_fusion.4
  146.7 0.2 maximum_maximum_fusion.1
  146.9 21.5 %all_to_all.31 = bf16[16,48,128]{2,1,0:T(8,128)(2,1)S(1)} all-to-all(bf16[16,48,128]{2,1,0:T(8,128)(2,1)S(1)} %maximum_maximum_fusion.1), channel_id=1, replica_groups=mesh['hist'=16,'rows_0'=4,'rows_1'=4,'rows_2'=2] {'hist'}, dimensions={0} | all-to-all | bytes 393216 | tf_op jit(solution)/shard_map/all_to_all | solution.py:121
  168.5 0.6 slice_reduce_fusion.1
  169.1 0.6 slice_reduce_fusion.5
  170.6 0.7 fusion.18
  175.8 0.6 stack_broadcast_in_dim.67
  176.4 0.7 stack_broadcast_in_dim.68
  177.1 1.9 collective-permute-start.2
  179.1 4.6 %collective-permute-done.2 = bf16[48,128]{1,0:T(8,128)(2,1)S(1)} collective-permute-done((bf16[48,128]{1,0:T(8,128)(2,1)S(1)}, bf16[48,128]{1,0:T(8,128)(2,1)S(1)}, u32[]{:S(2)}, u32[]{:S(2)}) %collective-permute-start.2) | collective-permute-done | bytes 12320 | tf_op jit(solution)/shard_map/ppermute | solution.py:101
  183.7 23.4 %all_to_all.32 = bf16[32,48,128]{2,1,0:T(8,128)(2,1)S(1)} all-to-all(bf16[32,48,128]{2,1,0:T(8,128)(2,1)S(1)} %broadcast_in_dim.48), channel_id=1, replica_groups=mesh['hist'=16,'rows_0'=4,'rows_1'=4,'rows_2'=2] {'rows_0','rows_1','row..., dimensions={0} | all-to-all | bytes 786432 | tf_op jit(solution)/shard_map/all_to_all | solution.py:103
  207.1 0.6 slice_reduce_fusion.4
  207.8 0.6 slice_reduce_fusion
  211.5 0.3 reshape.151
  211.9 0.5 copy.221
  212.4 0.7 reshape.161
  213.1 3.4 %fusion.8 = f32[2,64,11,128]{3,1,2,0:T(8,128)S(1)} fusion(bf16[11,128,1408,1]{2,1,0,3:T(8,128)(2,1)} %bitcast.91, bf16[2,64,1408,1]{2,1,0,3:T(8,128)(2,1)S(1)} %reshape.161), kind=kOutput, calls=%fused_computation.21 | convolution fusion | flops 507510784 | bytes 5046272 | tf_op jit(solution)/shard_map/dot_general | solution.py:109
  216.4 0.3 fusion.3
  217.7 1.4 maximum_maximum_fusion.3
  219.1 0.8 maximum_maximum_fusion.2
  219.9 6.0 %all-to-all-start.5 = ((bf16[16,48,128]{2,1,0:T(8,128)(2,1)}), bf16[16,48,128]{2,1,0:T(8,128)(2,1)S(1)}, u32[]{:S(2)}, u32[]{:S(2)}) async-start(bf16[16,48,128]{2,1,0:T(8,128)(2,1)} %maximum_maximum_fusion.2), calls=%async_computation.5 | async-start | bytes 393216 | tf_op jit(solution)/shard_map/all_to_all | solution.py:121
  225.9 16.7 %all-to-all-done.5 = bf16[16,48,128]{2,1,0:T(8,128)(2,1)S(1)} async-done(((bf16[16,48,128]{2,1,0:T(8,128)(2,1)}), bf16[16,48,128]{2,1,0:T(8,128)(2,1)S(1)}, u32[]{:S(2)}, u32[]{:S(2)}) %all-to-all-start.5) | async-done | bytes 196640 | tf_op jit(solution)/shard_map/all_to_all | solution.py:121
  242.8 0.6 convert_reduce_fusion.3
  244.2 0.7 maximum_add_fusion.2
  (94 shorter events, 4.1 us)
Async XLA Ops:
  0.6 49.9 %copy-start = (f32[64,64]{1,0:T(8,128)S(1)}, f32[64,64]{1,0:T(8,128)}, u32[]{:S(2)}) copy-start(f32[64,64]{1,0:T(8,128)} %param.10) | copy-start | bytes 49156
  9.3 6.5 %collective-permute-start = (bf16[48,128]{1,0:T(8,128)(2,1)S(1)}, bf16[48,128]{1,0:T(8,128)(2,1)S(1)}, u32[]{:S(2)}, u32[]{:S(2)}) collective-permute-start(bf16[48,128]{1,0:T(8,128)(2,1)S(1)} %concatenate.87), channel_id=1, source_target_pairs={{0,0},{1,1},{2,32},{3,33},{4,64},{5,65},{6,96},{7,97},{8,128},{9,1... | collective-permute-start | bytes 36872 | tf_op jit(solution)/shard_map/ppermute | solution.py:101
  16.6 33.9 %all-to-all-start = ((bf16[32,48,128]{2,1,0:T(8,128)(2,1)}), bf16[32,48,128]{2,1,0:T(8,128)(2,1)S(1)}, u32[]{:S(2)}, u32[]{:S(2)}) async-start(bf16[32,48,128]{2,1,0:T(8,128)(2,1)} %broadcast_in_dim.22), calls=%async_computation | async-start | bytes 786432 | tf_op jit(solution)/shard_map/all_to_all | solution.py:103
  56.6 19.9 %copy-start.1 = (f32[64,11,128]{2,0,1:T(8,128)S(1)}, f32[64,11,128]{2,0,1:T(8,128)}, u32[]{:S(2)}) copy-start(f32[64,11,128]{2,0,1:T(8,128)} %param.7) | copy-start | bytes 1081348
  56.6 19.9 %copy-start.2 = (f32[64,11,128]{2,0,1:T(8,128)S(1)}, f32[64,11,128]{2,0,1:T(8,128)}, u32[]{:S(2)}) copy-start(f32[64,11,128]{2,0,1:T(8,128)} %param.8) | copy-start | bytes 1081348
  63.6 29.2 %all-to-all-start.1 = ((bf16[16,48,128]{2,1,0:T(8,128)(2,1)}), bf16[16,48,128]{2,1,0:T(8,128)(2,1)S(1)}, u32[]{:S(2)}, u32[]{:S(2)}) async-start(bf16[16,48,128]{2,1,0:T(8,128)(2,1)} %maximum_maximum_fusion), calls=%async_computation.1 | async-start | bytes 393216 | tf_op jit(solution)/shard_map/all_to_all | solution.py:121
  100.4 6.5 %collective-permute-start.1 = (bf16[48,128]{1,0:T(8,128)(2,1)S(1)}, bf16[48,128]{1,0:T(8,128)(2,1)S(1)}, u32[]{:S(2)}, u32[]{:S(2)}) collective-permute-start(bf16[48,128]{1,0:T(8,128)(2,1)S(1)} %concatenate.94), channel_id=1, source_target_pairs={{0,0},{1,1},{2,32},{3,33},{4,64},{5,65},{6,96},{7,97},{8,128},{9,1... | collective-permute-start | bytes 36872 | tf_op jit(solution)/shard_map/ppermute | solution.py:101
  177.1 6.5 %collective-permute-start.2 = (bf16[48,128]{1,0:T(8,128)(2,1)S(1)}, bf16[48,128]{1,0:T(8,128)(2,1)S(1)}, u32[]{:S(2)}, u32[]{:S(2)}) collective-permute-start(bf16[48,128]{1,0:T(8,128)(2,1)S(1)} %concatenate.101), channel_id=1, source_target_pairs={{0,0},{1,1},{2,32},{3,33},{4,64},{5,65},{6,96},{7,97},{8,128},{9,1... | collective-permute-start | bytes 36872 | tf_op jit(solution)/shard_map/ppermute | solution.py:101
  219.9 22.7 %all-to-all-start.5 = ((bf16[16,48,128]{2,1,0:T(8,128)(2,1)}), bf16[16,48,128]{2,1,0:T(8,128)(2,1)S(1)}, u32[]{:S(2)}, u32[]{:S(2)}) async-start(bf16[16,48,128]{2,1,0:T(8,128)(2,1)} %maximum_maximum_fusion.2), calls=%async_computation.5 | async-start | bytes 393216 | tf_op jit(solution)/shard_map/all_to_all | solution.py:121
  244.1 0.8 copy-start.3

commit v2 on v1

v2 whole, which is shorter than its diff:
```python
import functools

import jax
import jax.numpy as jnp
from jax import lax
from jax.experimental import pallas as pl
from jax.experimental.pallas import tpu as pltpu
from jax.sharding import Mesh
from jax.sharding import PartitionSpec as P

ITERS = 3
ROWS = ("rows_0", "rows_1", "rows_2")
EVERY = ("hist", "rows_0", "rows_1", "rows_2")
SMALL = 2.0**-90
LARGE = 2.0**90
FAR = 2.0**13

step_size = 0.5
half_step = 0.25


def low_half(shape):
    return lax.broadcasted_iota(jnp.int32, shape, len(shape) - 1) < shape[-1] // 2


def swapped(value):
    return pltpu.roll(value, value.shape[-1] // 2, axis=value.ndim - 1)


def notes(row, first, power, peak):
    high = power.astype(jnp.bfloat16).astype(jnp.float32)
    parts = (high, power - high, peak)
    value = jnp.zeros(row.shape, jnp.float32)
    for at, part in enumerate(parts):
        value = jnp.where(row == first + at, part, value)
    return value


def write_piece(piece_ref, field, factor_ref, mask_ref, damping, cells):
    row = lax.broadcasted_iota(jnp.int32, field.shape, 0)
    square = field * field
    square = square + swapped(square)
    power = jnp.sum(square * mask_ref[...], axis=(0, 1), keepdims=True)
    peak = jnp.max(jnp.where(row < cells, square, 0.0), axis=(0, 1), keepdims=True)
    sigma = factor_ref[...] * (square * damping) * field
    piece_ref[...] = jnp.where(row < cells, sigma, notes(row, cells, power, peak)).astype(
        piece_ref.dtype
    )


def first_kernel(field_ref, factor_ref, mask_ref, piece_ref, *, cells):
    write_piece(piece_ref, field_ref[...], factor_ref, mask_ref, 1.0, cells)


def advance(arrived_ref, base_ref, restore, cells, total_cells):
    arrived = arrived_ref[...].astype(jnp.float32)
    total = jnp.sum(arrived, axis=0)
    row = lax.broadcasted_iota(jnp.int32, total.shape, 0)
    marked = (row == cells) | (row == cells + 1)
    power = jnp.sum(jnp.where(marked, total, 0.0), axis=0, keepdims=True)
    peak = jnp.max(jnp.where(row == cells + 2, jnp.max(arrived, axis=0), 0.0), axis=0, keepdims=True)
    integral = total / (1.0 + power / total_cells)
    if restore is not None:
        integral = integral * restore
    sign = jnp.where(low_half(total.shape), half_step, -half_step)
    return integral, base_ref[...] + swapped(integral) * sign, peak


def next_kernel(arrived_ref, base_ref, factor_ref, mask_ref, piece_ref, *, cells, total_cells):
    field = advance(arrived_ref, base_ref, None, cells, total_cells)[1]
    write_piece(piece_ref, field, factor_ref, mask_ref, 1.0, cells)


def guarded_kernel(
    arrived_ref, base_ref, factor_ref, mask_ref, piece_ref, restore_ref, *, cells, total_cells
):
    _, field, peak = advance(arrived_ref, base_ref, None, cells, total_cells)
    damping = jnp.where(peak > FAR, SMALL, 1.0)
    restore_ref[...] = jnp.broadcast_to(jnp.where(peak > FAR, LARGE, 1.0), restore_ref.shape)
    write_piece(piece_ref, field, factor_ref, mask_ref, damping, cells)


def last_kernel(arrived_ref, base_ref, restore_ref, row_ref, integral_ref, *, cells, total_cells):
    integral, field, _ = advance(arrived_ref, base_ref, restore_ref[0:1], cells, total_cells)
    row_ref[...] = field[:cells]
    integral_ref[...] = integral[:cells]


def contract_kernel(pieces_ref, history_ref, out_ref, field_ref, left_ref, terms_ref, *, times):
    count, padded, wide = pieces_ref.shape
    groups = padded // 8
    shares = count // 2
    orbits = wide // 2
    upper = lax.broadcasted_iota(jnp.int32, (groups, 8, wide), 1) < 4
    for k in range(2):
        for v in range(shares // 2):
            first = pieces_ref[4 * v + k].astype(jnp.float32).reshape(groups, 8, wide)
            second = pieces_ref[4 * v + 2 + k].astype(jnp.float32).reshape(groups, 8, wide)
            even = jnp.where(upper, first, pltpu.roll(second, 4, axis=1))
            odd = jnp.where(upper, pltpu.roll(first, 4, axis=1), second)
            field_ref[k, 0, :, 8 * v : 8 * v + 8, :] = even
            field_ref[k, 1, :, 8 * v : 8 * v + 8, :] = odd
    low = low_half((orbits, wide))
    for pair in range(times):
        blocks = []
        for s in (2 * pair, 2 * pair + 1):
            k, t = divmod(s, times)
            blocks.append(field_ref[k, t % 2, t // 2])
        lanes = slice(pair * wide, (pair + 1) * wide)
        left_ref[:orbits, lanes] = jnp.where(low, blocks[0], swapped(blocks[1])).astype(jnp.bfloat16)
        left_ref[orbits:, lanes] = jnp.where(low, swapped(blocks[0]), blocks[1]).astype(jnp.bfloat16)
    left = left_ref[...]
    depth = left.shape[1]
    sign = jnp.where(low, -1.0, 1.0)
    which = lax.broadcasted_iota(jnp.int32, (orbits, wide), 0) % 4
    marks = [field_ref[k, 1, groups - 1] for k in range(2)]
    power = jnp.sum(jnp.where(which < 2, marks[0] + marks[1], 0.0), axis=0, keepdims=True)
    peak = jnp.max(
        jnp.where(which == 2, jnp.maximum(marks[0], marks[1]), 0.0), axis=0, keepdims=True
    )
    upper = lax.broadcasted_iota(jnp.int32, (orbits // 8, 8, wide), 1) < 4
    for pair in range(groups):
        moments = [t for t in (2 * pair, 2 * pair + 1) if t < times]
        right = [history_ref[:, t].reshape(depth, wide) for t in moments]
        right = jnp.concatenate(right, -1) if len(right) > 1 else right[0]
        product = jnp.dot(left, right, preferred_element_type=jnp.float32)
        values = []
        for at in range(len(moments)):
            lanes = slice(at * wide, (at + 1) * wide)
            values.append(product[:orbits, lanes] + swapped(product[orbits:, lanes]) * sign)
        if len(moments) < 2:
            values.append(notes(which, 0, power, peak))
        even, odd = (value.reshape(orbits // 8, 8, wide) for value in values)
        terms_ref[:, 0, pair] = jnp.where(upper, even, pltpu.roll(odd, 4, axis=1))
        terms_ref[:, 1, pair] = jnp.where(upper, pltpu.roll(even, 4, axis=1), odd)
    out_ref[...] = terms_ref[...].reshape(shares, padded, wide).astype(out_ref.dtype)


def on_device(g_hist, g_last, integral_last, coupling, step_re, step_im):
    orbits = g_last.shape[0]
    row_count = g_last.shape[1]
    wide = 2 * orbits
    hist_size = lax.axis_size("hist")
    rows_size = lax.axis_size(ROWS)
    fan_out = rows_size // hist_size
    hist_at = lax.axis_index("hist")
    rows_at = lax.axis_index(ROWS)
    total_cells = row_count * rows_size * orbits
    share = orbits // hist_size
    cells = share * row_count
    padded = cells + share
    swap = [
        ((z * hist_size + p) * fan_out + k, (p * hist_size + z) * fan_out + k)
        for z in range(hist_size)
        for p in range(hist_size)
        for k in range(fan_out)
    ]

    def my_rows(whole):
        return lax.dynamic_slice_in_dim(whole, hist_at * share, share, 0)

    def as_rows(value):
        value = value.transpose(1, 0, 2).reshape(cells, wide)
        return jnp.pad(value, ((0, padded - cells), (0, 0)))

    moments = rows_at * row_count + jnp.arange(row_count)
    weights = step_size * jnp.where(moments == 0, 0.5, 1.0).astype(jnp.float32)
    coupling_part = my_rows(coupling)
    twice = jnp.concatenate([coupling_part, coupling_part], -1)
    factor = as_rows(twice[:, None, :] * weights[None, :, None])
    row = jnp.arange(padded)[:, None]
    own = (row % share + hist_at * share == jnp.arange(wide)[None, :]) & (row < cells)
    mask = own.astype(jnp.float32)
    shifted = jnp.concatenate(
        [
            g_last[..., :orbits] + half_step * integral_last[..., orbits:],
            g_last[..., orbits:] - half_step * integral_last[..., :orbits],
        ],
        -1,
    )
    steps = jnp.concatenate([my_rows(step_re), my_rows(step_im)], 0)
    moved = lax.dot_general(
        steps,
        shifted,
        (((1,), (0,)), ((), ())),
        precision=lax.Precision.HIGHEST,
        preferred_element_type=jnp.float32,
    ).reshape(2, share, row_count, wide)
    base = as_rows(
        jnp.concatenate(
            [
                moved[0, ..., :orbits] - moved[1, ..., orbits:],
                moved[0, ..., orbits:] + moved[1, ..., :orbits],
            ],
            -1,
        )
    )
    history = g_hist.transpose(0, 2, 1, 3)
    piece_shape = jax.ShapeDtypeStruct((padded, wide), jnp.bfloat16)
    row_shape = jax.ShapeDtypeStruct((cells, wide), jnp.float32)
    sizes = {"cells": cells, "total_cells": total_cells}
    piece = pl.pallas_call(functools.partial(first_kernel, cells=cells), out_shape=piece_shape)(
        as_rows(my_rows(g_last)), factor, mask
    )
    contract = pl.pallas_call(
        functools.partial(contract_kernel, times=row_count),
        out_shape=jax.ShapeDtypeStruct((hist_size, padded, wide), jnp.bfloat16),
        scratch_shapes=[
            pltpu.VMEM((fan_out, 2, padded // 8, orbits, wide), jnp.float32),
            pltpu.VMEM((wide, fan_out * row_count * orbits), jnp.bfloat16),
            pltpu.VMEM((hist_size // 2, 2, padded // 8, 8, wide), jnp.float32),
        ],
    )
    for iteration in range(ITERS):
        piece = lax.ppermute(piece, EVERY, swap)
        copies = jnp.broadcast_to(piece[None], (rows_size, padded, wide))
        pieces = lax.all_to_all(copies, ROWS, split_axis=0, concat_axis=0, tiled=True)
        sent = contract(pieces, history)
        arrived = lax.all_to_all(sent, "hist", split_axis=0, concat_axis=0, tiled=True)
        if iteration == 0:
            piece = pl.pallas_call(functools.partial(next_kernel, **sizes), out_shape=piece_shape)(
                arrived, base, factor, mask
            )
        elif iteration == 1:
            piece, restore = pl.pallas_call(
                functools.partial(guarded_kernel, **sizes),
                out_shape=(piece_shape, jax.ShapeDtypeStruct((8, wide), jnp.float32)),
            )(arrived, base, factor, mask)
        else:
            new_row, new_integral = pl.pallas_call(
                functools.partial(last_kernel, **sizes), out_shape=(row_shape, row_shape)
            )(arrived, base, restore)

    def as_output(rows):
        return rows.reshape(row_count, share, wide).transpose(1, 0, 2)

    return as_output(new_row), as_output(new_integral)


def solution(mesh):
    split = Mesh(
        mesh.devices.reshape(mesh.shape["hist"], 4, 4, 2), ("hist", "rows_0", "rows_1", "rows_2")
    )
    return jax.shard_map(
        on_device,
        mesh=split,
        in_specs=(
            P("hist", None, ROWS, None),
            P(None, ROWS, None),
            P(None, ROWS, None),
            P(),
            P(),
            P(),
        ),
        out_specs=(P("hist", ROWS, None), P("hist", ROWS, None)),
        check_vma=False,
    )
```

time: 246 us -> 198 us (0.80)
  blocking collectives: 72.5 us -> 121 us
  between operations: 25.6 us -> 0.76 us
  starting transfers between devices: 44.5 us -> 19.7 us
  local copies, waits for them, and re-layouts: 28.9 us -> 7.79 us
  Pallas kernels: 0 us -> 18.5 us
  other arithmetic: 18.7 us -> 1.27 us
  waiting for transfers between devices: 44 us -> 27.8 us
  matrix products: 10.6 us -> 0.4 us
    all_to_all x1 -> x2, blocking collectives: 21.5 us -> 46.6 us  [on_device(): lax.all_to_all(sent, 'hist', split_axis=0, concat_axis=0, tiled=True)]
    all_to_all x2 -> x3, blocking collectives: 51 us -> 74.5 us  [on_device(): lax.all_to_all(copies, ROWS, split_axis=0, concat_axis=0, tiled=True)]
    pallas_call x0 -> x7, Pallas kernels: none -> 18.5 us  [the longest x3 11.6 us: on_device(): sent = contract(pieces, history)]
    all_to_all x1 -> x0, starting transfers between devices: 18 us -> none  [on_device(): lax.all_to_all(copies, ROWS, split_axis=0, concat_axis=0, tiled=True)]
    all_to_all x2 -> x1, waiting for transfers between devices: 32.2 us -> 14.5 us  [on_device(): lax.all_to_all(sent, 'hist', split_axis=0, concat_axis=0, tiled=True)]
    dot_general x4 -> x1, matrix products: 10.6 us -> 0.4 us  [on_device(): lax.dot_general(steps, shifted, (((1,), (0,)), ((), ())), precision=lax.P...]
    unnamed x18 -> x8, local copies, waits for them, and re-layouts: 9.99 us -> 1.39 us
    dot_general x4 -> x0, local copies, waits for them, and re-layouts: 8.29 us -> none  [on_device(): product = jnp.dot(left, history, preferred_element_type=jnp.float32)]
  transfers between devices with their start and end apart: 6 -> 4, of which waited for: 5 -> 4; matrix products, arithmetic and copies ran while one was open for 7% -> 1% of each run, Pallas kernels for 0% -> 0%
where the time goes in v2:
time: 198 us; the launch traced here: 197 us
  blocking collectives  121 us (61%)
  waiting for transfers between devices  27.8 us (14%)
  starting transfers between devices  19.7 us (10%)
  Pallas kernels  18.5 us (9%)
  local copies, waits for them, and re-layouts  7.79 us (4%)
    all_to_all x3, blocking collectives, on_device(): lax.all_to_all(copies, ROWS, split_axis=0, concat_axis=0, tiled=True)  74.5 us
    all_to_all x2, blocking collectives, on_device(): lax.all_to_all(sent, 'hist', split_axis=0, concat_axis=0, tiled=True)  46.6 us
    all_to_all x1, waiting for transfers between devices, on_device(): lax.all_to_all(sent, 'hist', split_axis=0, concat_axis=0, tiled=True)  14.5 us
    ppermute x3, waiting for transfers between devices, on_device(): piece = lax.ppermute(piece, EVERY, swap)  13.3 us
    all_to_all x1, starting transfers between devices, on_device(): lax.all_to_all(sent, 'hist', split_axis=0, concat_axis=0, tiled=True)  12.9 us
    pallas_call x3, Pallas kernels, on_device(): sent = contract(pieces, history)  11.6 us
    ppermute x3, starting transfers between devices, on_device(): piece = lax.ppermute(piece, EVERY, swap)  6.83 us
  transfers between devices with their start and end apart: 4, of which 4 were waited for; matrix products, arithmetic and copies ran while one was open for 1% of the time, Pallas kernels for 0%

profile of v2, /device:TPU:32, one launch (start us, length us, event | category | flops | bytes accessed | tf_op | source)
XLA Modules:
  0.0 197.4 jit_solution(436756481859402739)
XLA Ops:
  0.6 0.0 copy-start
  0.6 0.0 copy-start.1
  0.7 0.0 copy-start.2
  0.7 0.7 copy-done
  1.4 0.1 pad_maximum_fusion
  1.5 0.1 mul.57
  1.6 0.1 mul.58
  1.7 0.8 dynamic-slice_bitcast_fusion
  2.5 0.1 broadcast_multiply_fusion
  2.6 0.6 pad.11.factor_ref
  3.2 0.6 pad.10.field_ref
  3.8 0.7 fusion.5.mask_ref
  4.5 1.6 shard_map.77
  6.0 3.0 %collective-permute-start = (bf16[48,128]{1,0:T(8,128)(2,1)}, bf16[48,128]{1,0:T(8,128)(2,1)S(1)}, u32[]{:S(2)}, u32[]{:S(2)}) collective-permute-start(bf16[48,128]{1,0:T(8,128)(2,1)} %shard_map.77), channel_id=1, source_target_pairs={{0,0},{1,1},{2,32},{3,33},{4,64},{5,65},{6,96},{7,97},{8,128},{9,1... | collective-permute-start | bytes 36872 | tf_op jit(solution)/shard_map/ppermute | solution.py:215
  9.1 3.7 %collective-permute-done = bf16[48,128]{1,0:T(8,128)(2,1)S(1)} collective-permute-done((bf16[48,128]{1,0:T(8,128)(2,1)}, bf16[48,128]{1,0:T(8,128)(2,1)S(1)}, u32[]{:S(2)}, u32[]{:S(2)}) %collective-permute-start) | collective-permute-done | bytes 12320 | tf_op jit(solution)/shard_map/ppermute | solution.py:215
  12.7 0.1 broadcast_in_dim.16
  12.8 27.9 %all_to_all.30.pieces_ref = bf16[32,48,128]{2,1,0:T(8,128)(2,1)} all-to-all(bf16[32,48,128]{2,1,0:T(8,128)(2,1)S(1)} %broadcast_in_dim.16), channel_id=1, replica_groups=mesh['hist'=16,'rows_0'=4,'rows_1'=4,'rows_2'=2] {'rows_0','rows_1','row..., dimensions={0} | all-to-all | bytes 786432 | tf_op jit(solution)/shard_map/all_to_all | solution.py:217
  40.7 3.9 %shard_map.78 = bf16[16,48,128]{2,1,0:T(8,128)(2,1)} custom-call(bf16[32,48,128]{2,1,0:T(8,128)(2,1)} %all_to_all.30.pieces_ref, bf16[22,11,64,128]{3,2,1,0:T(8,128)(2,1)} %bitcast.35), custom_call_target="tpu_custom_call" | custom-call | tf_op jit(solution)/shard_map/pallas_call | solution.py:218
  44.5 12.9 %all-to-all-start.1 = ((bf16[16,48,128]{2,1,0:T(8,128)(2,1)}), bf16[16,48,128]{2,1,0:T(8,128)(2,1)S(1)}, u32[]{:S(2)}, u32[]{:S(2)}) async-start(bf16[16,48,128]{2,1,0:T(8,128)(2,1)} %shard_map.78), calls=%async_computation.1 | async-start | bytes 393216 | tf_op jit(solution)/shard_map/all_to_all | solution.py:219
  57.4 0.7 constant_dynamic-slice_fusion
  58.1 0.0 copy-done.1
  58.1 0.0 copy-done.2
  58.1 0.3 multiply_add_fusion
  58.4 0.4 fusion
  58.8 0.1 fusion.9
  58.9 0.1 maximum_bitcast_fusion
  59.0 0.6 pad.12.base_ref
  59.6 14.5 %all-to-all-done.1.arrived_ref = bf16[16,48,128]{2,1,0:T(8,128)(2,1)S(1)} async-done(((bf16[16,48,128]{2,1,0:T(8,128)(2,1)}), bf16[16,48,128]{2,1,0:T(8,128)(2,1)S(1)}, u32[]{:S(2)}, u32[]{:S(2)}) %all-to-all-start.1) | async-done | bytes 196640 | tf_op jit(solution)/shard_map/all_to_all | solution.py:219
  74.1 0.0 copy-start.3
  74.1 0.7 copy-done.3
  74.8 1.8 shard_map.79
  76.6 1.9 collective-permute-start.1
  78.5 4.8 %collective-permute-done.1 = bf16[48,128]{1,0:T(8,128)(2,1)S(1)} collective-permute-done((bf16[48,128]{1,0:T(8,128)(2,1)}, bf16[48,128]{1,0:T(8,128)(2,1)S(1)}, u32[]{:S(2)}, u32[]{:S(2)}) %collective-permute-start.1) | collective-permute-done | bytes 12320 | tf_op jit(solution)/shard_map/ppermute | solution.py:215
  83.3 0.1 broadcast_in_dim.17
  83.4 23.5 %all_to_all.31.pieces_ref = bf16[32,48,128]{2,1,0:T(8,128)(2,1)} all-to-all(bf16[32,48,128]{2,1,0:T(8,128)(2,1)S(1)} %broadcast_in_dim.17), channel_id=1, replica_groups=mesh['hist'=16,'rows_0'=4,'rows_1'=4,'rows_2'=2] {'rows_0','rows_1','row..., dimensions={0} | all-to-all | bytes 786432 | tf_op jit(solution)/shard_map/all_to_all | solution.py:217
  106.8 3.9 %shard_map.80 = bf16[16,48,128]{2,1,0:T(8,128)(2,1)} custom-call(bf16[32,48,128]{2,1,0:T(8,128)(2,1)} %all_to_all.31.pieces_ref, bf16[22,11,64,128]{3,2,1,0:T(8,128)(2,1)} %bitcast.36), custom_call_target="tpu_custom_call" | custom-call | tf_op jit(solution)/shard_map/pallas_call | solution.py:218
  110.7 23.2 %all_to_all.32.arrived_ref = bf16[16,48,128]{2,1,0:T(8,128)(2,1)} all-to-all(bf16[16,48,128]{2,1,0:T(8,128)(2,1)} %shard_map.80), channel_id=1, replica_groups=mesh['hist'=16,'rows_0'=4,'rows_1'=4,'rows_2'=2] {'hist'}, dimensions={0} | all-to-all | bytes 393216 | tf_op jit(solution)/shard_map/all_to_all | solution.py:219
  133.9 1.9 shard_map.81
  135.8 1.9 collective-permute-start.2
  137.7 4.9 %collective-permute-done.2 = bf16[48,128]{1,0:T(8,128)(2,1)S(1)} collective-permute-done((bf16[48,128]{1,0:T(8,128)(2,1)}, bf16[48,128]{1,0:T(8,128)(2,1)S(1)}, u32[]{:S(2)}, u32[]{:S(2)}) %collective-permute-start.2) | collective-permute-done | bytes 12320 | tf_op jit(solution)/shard_map/ppermute | solution.py:215
  142.6 0.1 broadcast_in_dim.18
  142.6 23.2 %all_to_all.33.pieces_ref = bf16[32,48,128]{2,1,0:T(8,128)(2,1)} all-to-all(bf16[32,48,128]{2,1,0:T(8,128)(2,1)S(1)} %broadcast_in_dim.18), channel_id=1, replica_groups=mesh['hist'=16,'rows_0'=4,'rows_1'=4,'rows_2'=2] {'rows_0','rows_1','row..., dimensions={0} | all-to-all | bytes 786432 | tf_op jit(solution)/shard_map/all_to_all | solution.py:217
  165.8 3.9 %shard_map.82 = bf16[16,48,128]{2,1,0:T(8,128)(2,1)} custom-call(bf16[32,48,128]{2,1,0:T(8,128)(2,1)} %all_to_all.33.pieces_ref, bf16[22,11,64,128]{3,2,1,0:T(8,128)(2,1)} %bitcast.37), custom_call_target="tpu_custom_call" | custom-call | tf_op jit(solution)/shard_map/pallas_call | solution.py:218
  169.7 23.4 %all_to_all.34.arrived_ref = bf16[16,48,128]{2,1,0:T(8,128)(2,1)} all-to-all(bf16[16,48,128]{2,1,0:T(8,128)(2,1)} %shard_map.82), channel_id=1, replica_groups=mesh['hist'=16,'rows_0'=4,'rows_1'=4,'rows_2'=2] {'hist'}, dimensions={0} | all-to-all | bytes 393216 | tf_op jit(solution)/shard_map/all_to_all | solution.py:219
  193.0 1.7 shard_map.83
  194.7 1.4 reshape.60
  196.1 1.4 reshape.61
  (8 shorter events, 0.1 us)
Async XLA Ops:
  0.6 0.8 copy-start
  0.6 57.5 %copy-start.1 = (f32[64,11,128]{2,0,1:T(8,128)S(1)}, f32[64,11,128]{2,0,1:T(8,128)}, u32[]{:S(2)}) copy-start(f32[64,11,128]{2,0,1:T(8,128)} %param.7) | copy-start | bytes 1081348
  0.7 57.5 %copy-start.2 = (f32[64,11,128]{2,0,1:T(8,128)S(1)}, f32[64,11,128]{2,0,1:T(8,128)}, u32[]{:S(2)}) copy-start(f32[64,11,128]{2,0,1:T(8,128)} %param.8) | copy-start | bytes 1081348
  6.0 6.7 %collective-permute-start = (bf16[48,128]{1,0:T(8,128)(2,1)}, bf16[48,128]{1,0:T(8,128)(2,1)S(1)}, u32[]{:S(2)}, u32[]{:S(2)}) collective-permute-start(bf16[48,128]{1,0:T(8,128)(2,1)} %shard_map.77), channel_id=1, source_target_pairs={{0,0},{1,1},{2,32},{3,33},{4,64},{5,65},{6,96},{7,97},{8,128},{9,1... | collective-permute-start | bytes 36872 | tf_op jit(solution)/shard_map/ppermute | solution.py:215
  44.5 29.6 %all-to-all-start.1 = ((bf16[16,48,128]{2,1,0:T(8,128)(2,1)}), bf16[16,48,128]{2,1,0:T(8,128)(2,1)S(1)}, u32[]{:S(2)}, u32[]{:S(2)}) async-start(bf16[16,48,128]{2,1,0:T(8,128)(2,1)} %shard_map.78), calls=%async_computation.1 | async-start | bytes 393216 | tf_op jit(solution)/shard_map/all_to_all | solution.py:219
  74.1 0.7 copy-start.3
  76.6 6.7 %collective-permute-start.1 = (bf16[48,128]{1,0:T(8,128)(2,1)}, bf16[48,128]{1,0:T(8,128)(2,1)S(1)}, u32[]{:S(2)}, u32[]{:S(2)}) collective-permute-start(bf16[48,128]{1,0:T(8,128)(2,1)} %shard_map.79), channel_id=1, source_target_pairs={{0,0},{1,1},{2,32},{3,33},{4,64},{5,65},{6,96},{7,97},{8,128},{9,1... | collective-permute-start | bytes 36872 | tf_op jit(solution)/shard_map/ppermute | solution.py:215
  135.8 6.8 %collective-permute-start.2 = (bf16[48,128]{1,0:T(8,128)(2,1)}, bf16[48,128]{1,0:T(8,128)(2,1)S(1)}, u32[]{:S(2)}, u32[]{:S(2)}) collective-permute-start(bf16[48,128]{1,0:T(8,128)(2,1)} %get-tuple-element.6), channel_id=1, source_target_pairs={{0,0},{1,1},{2,32},{3,33},{4,64},{5,65},{6,96},{7,97},{8,128},{9,1... | collective-permute-start | bytes 36872 | tf_op jit(solution)/shard_map/ppermute | solution.py:215

commit v3 on v2

--- a/solution.py
+++ b/solution.py
@@ -17,6 +17,35 @@
 
 step_size = 0.5
 half_step = 0.25
+
+
+SCALARS = pl.BlockSpec(memory_space=pltpu.SMEM)
+VECTORS = pl.BlockSpec(memory_space=pltpu.VMEM)
+
+
+def call(kernel, shape, specs, scratch=()):
+    outs = (VECTORS,) * len(shape) if isinstance(shape, tuple) else VECTORS
+    return pl.pallas_call(
+        kernel, out_shape=shape, in_specs=specs, out_specs=outs, scratch_shapes=list(scratch)
+    )
+
+
+def places(hist_size):
+    side = round(hist_size**0.5)
+
+    def ring(a, b, size):
+        return min((a - b) % size, (b - a) % size)
+
+    spots = []
+    for p in range(hist_size):
+        far_first = sorted(range(hist_size), key=lambda z: (-ring(z, p, hist_size), z))
+        near_first = sorted(
+            range(hist_size),
+            key=lambda q: (ring(q // side, p // side, side) + ring(q % side, p % side, side), q),
+        )
+        at = dict(zip(far_first, near_first))
+        spots.append([at[z] for z in range(hist_size)])
+    return spots
 
 
 def low_half(shape):
@@ -48,8 +77,37 @@
     )
 
 
-def first_kernel(field_ref, factor_ref, mask_ref, piece_ref, *, cells):
-    write_piece(piece_ref, field_ref[...], factor_ref, mask_ref, 1.0, cells)
+def first_kernel(
+    at_ref, rows_ref, coupling_ref, piece_ref, factor_ref, mask_ref, *, cells, share
+):
+    hist_at, rows_at = at_ref[0], at_ref[1]
+    padded, wide = factor_ref.shape
+    groups = padded // 8
+    start = pl.multiple_of(hist_at // 2 * 8, 8)
+    late = hist_at % 2 == 1
+    row = lax.broadcasted_iota(jnp.int32, (8, wide), 0)
+    lane = lax.broadcasted_iota(jnp.int32, (8, wide), 1)
+    upper = row < share
+
+    def doubled(even, odd):
+        up = jnp.where(late, pltpu.roll(even, 4, axis=0), even)
+        down = jnp.where(late, odd, pltpu.roll(odd, 4, axis=0))
+        return jnp.where(upper, up, down)
+
+    own = coupling_ref[pl.ds(start, 8), :]
+    factor = doubled(own, own) * step_size
+    mask = jnp.where(lane == hist_at * share + row % share, 1.0, 0.0)
+    field = []
+    for group in range(groups):
+        even = rows_ref[2 * group, pl.ds(start, 8), :]
+        last = 2 * group + 1 == rows_ref.shape[0]
+        odd = jnp.zeros_like(even) if last else rows_ref[2 * group + 1, pl.ds(start, 8), :]
+        field.append(doubled(even, odd))
+        scaled = jnp.where(upper & (rows_at == 0), factor * 0.5, factor) if group == 0 else factor
+        factor_ref[8 * group : 8 * group + 8, :] = jnp.where(upper, scaled, 0.0) if last else scaled
+        mask_ref[8 * group : 8 * group + 8, :] = jnp.where(upper, mask, 0.0) if last else mask
+    field = jnp.concatenate(field, 0)
+    write_piece(piece_ref, field, factor_ref, mask_ref, 1.0, cells)
 
 
 def advance(arrived_ref, base_ref, restore, cells, total_cells):
@@ -82,11 +140,13 @@
 
 def last_kernel(arrived_ref, base_ref, restore_ref, row_ref, integral_ref, *, cells, total_cells):
     integral, field, _ = advance(arrived_ref, base_ref, restore_ref[0:1], cells, total_cells)
-    row_ref[...] = field[:cells]
-    integral_ref[...] = integral[:cells]
-
-
-def contract_kernel(pieces_ref, history_ref, out_ref, field_ref, left_ref, terms_ref, *, times):
+    times, share, _ = row_ref.shape
+    for t in range(times):
+        row_ref[t] = field[t * share : (t + 1) * share]
+        integral_ref[t] = integral[t * share : (t + 1) * share]
+
+
+def contract_kernel(order_ref, pieces_ref, history_ref, out_ref, field_ref, left_ref, terms_ref, *, times):
     count, padded, wide = pieces_ref.shape
     groups = padded // 8
     shares = count // 2
@@ -94,8 +154,12 @@
     upper = lax.broadcasted_iota(jnp.int32, (groups, 8, wide), 1) < 4
     for k in range(2):
         for v in range(shares // 2):
-            first = pieces_ref[4 * v + k].astype(jnp.float32).reshape(groups, 8, wide)
-            second = pieces_ref[4 * v + 2 + k].astype(jnp.float32).reshape(groups, 8, wide)
+            first, second = (
+                pieces_ref[2 * order_ref[2 * v + at] + k]
+                .astype(jnp.float32)
+                .reshape(groups, 8, wide)
+                for at in range(2)
+            )
             even = jnp.where(upper, first, pltpu.roll(second, 4, axis=1))
             odd = jnp.where(upper, pltpu.roll(first, 4, axis=1), second)
             field_ref[k, 0, :, 8 * v : 8 * v + 8, :] = even
@@ -149,12 +213,14 @@
     share = orbits // hist_size
     cells = share * row_count
     padded = cells + share
+    spots = places(hist_size)
     swap = [
-        ((z * hist_size + p) * fan_out + k, (p * hist_size + z) * fan_out + k)
+        ((z * hist_size + p) * fan_out + k, (p * hist_size + spots[p][z]) * fan_out + k)
         for z in range(hist_size)
         for p in range(hist_size)
         for k in range(fan_out)
     ]
+    order = jnp.asarray(spots, jnp.int32)[hist_at]
 
     def my_rows(whole):
         return lax.dynamic_slice_in_dim(whole, hist_at * share, share, 0)
@@ -163,14 +229,6 @@
         value = value.transpose(1, 0, 2).reshape(cells, wide)
         return jnp.pad(value, ((0, padded - cells), (0, 0)))
 
-    moments = rows_at * row_count + jnp.arange(row_count)
-    weights = step_size * jnp.where(moments == 0, 0.5, 1.0).astype(jnp.float32)
-    coupling_part = my_rows(coupling)
-    twice = jnp.concatenate([coupling_part, coupling_part], -1)
-    factor = as_rows(twice[:, None, :] * weights[None, :, None])
-    row = jnp.arange(padded)[:, None]
-    own = (row % share + hist_at * share == jnp.arange(wide)[None, :]) & (row < cells)
-    mask = own.astype(jnp.float32)
     shifted = jnp.concatenate(
         [
             g_last[..., :orbits] + half_step * integral_last[..., orbits:],
@@ -197,15 +255,23 @@
     )
     history = g_hist.transpose(0, 2, 1, 3)
     piece_shape = jax.ShapeDtypeStruct((padded, wide), jnp.bfloat16)
-    row_shape = jax.ShapeDtypeStruct((cells, wide), jnp.float32)
+    local_shape = jax.ShapeDtypeStruct((padded, wide), jnp.float32)
+    row_shape = jax.ShapeDtypeStruct((row_count, share, wide), jnp.float32)
     sizes = {"cells": cells, "total_cells": total_cells}
-    piece = pl.pallas_call(functools.partial(first_kernel, cells=cells), out_shape=piece_shape)(
-        as_rows(my_rows(g_last)), factor, mask
-    )
-    contract = pl.pallas_call(
+    piece, factor, mask = call(
+        functools.partial(first_kernel, cells=cells, share=share),
+        (piece_shape, local_shape, local_shape),
+        (SCALARS, VECTORS, VECTORS),
+    )(
+        jnp.stack([hist_at, rows_at]).astype(jnp.int32),
+        g_last.transpose(1, 0, 2),
+        jnp.concatenate([coupling, coupling], -1),
+    )
+    contract = call(
         functools.partial(contract_kernel, times=row_count),
-        out_shape=jax.ShapeDtypeStruct((hist_size, padded, wide), jnp.bfloat16),
-        scratch_shapes=[
+        jax.ShapeDtypeStruct((hist_size, padded, wide), jnp.bfloat16),
+        (SCALARS, VECTORS, VECTORS),
+        [
             pltpu.VMEM((fan_out, 2, padded // 8, orbits, wide), jnp.float32),
             pltpu.VMEM((wide, fan_out * row_count * orbits), jnp.bfloat16),
             pltpu.VMEM((hist_size // 2, 2, padded // 8, 8, wide), jnp.float32),
@@ -215,26 +281,23 @@
         piece = lax.ppermute(piece, EVERY, swap)
         copies = jnp.broadcast_to(piece[None], (rows_size, padded, wide))
         pieces = lax.all_to_all(copies, ROWS, split_axis=0, concat_axis=0, tiled=True)
-        sent = contract(pieces, history)
+        sent = contract(order, pieces, history)
         arrived = lax.all_to_all(sent, "hist", split_axis=0, concat_axis=0, tiled=True)
         if iteration == 0:
-            piece = pl.pallas_call(functools.partial(next_kernel, **sizes), out_shape=piece_shape)(
+            piece = call(functools.partial(next_kernel, **sizes), piece_shape, (VECTORS,) * 4)(
                 arrived, base, factor, mask
             )
         elif iteration == 1:
-            piece, restore = pl.pallas_call(
+            piece, restore = call(
                 functools.partial(guarded_kernel, **sizes),
-                out_shape=(piece_shape, jax.ShapeDtypeStruct((8, wide), jnp.float32)),
+                (piece_shape, jax.ShapeDtypeStruct((8, wide), jnp.float32)),
+                (VECTORS,) * 4,
             )(arrived, base, factor, mask)
         else:
-            new_row, new_integral = pl.pallas_call(
-                functools.partial(last_kernel, **sizes), out_shape=(row_shape, row_shape)
+            new_row, new_integral = call(
+                functools.partial(last_kernel, **sizes), (row_shape, row_shape), (VECTORS,) * 3
             )(arrived, base, restore)
-
-    def as_output(rows):
-        return rows.reshape(row_count, share, wide).transpose(1, 0, 2)
-
-    return as_output(new_row), as_output(new_integral)
+    return new_row.transpose(1, 0, 2), new_integral.transpose(1, 0, 2)
 
 
 def solution(mesh):

time: 198 us -> 192 us (0.970)
  blocking collectives: 121 us -> 74.4 us
  waiting for transfers between devices: 27.8 us -> 56.1 us
  starting transfers between devices: 19.7 us -> 33.3 us
  local copies, waits for them, and re-layouts: 7.79 us -> 4.91 us
    all_to_all x3 -> x2, blocking collectives: 74.5 us -> 27.3 us  [on_device(): lax.all_to_all(copies, ROWS, split_axis=0, concat_axis=0, tiled=True)]
    ppermute x3, waiting for transfers between devices: 13.3 us -> 32.9 us  [on_device(): piece = lax.ppermute(piece, EVERY, swap)]
    all_to_all x0 -> x1, waiting for transfers between devices: none -> 8.76 us  [on_device(): lax.all_to_all(copies, ROWS, split_axis=0, concat_axis=0, tiled=True)]
    ppermute x3, starting transfers between devices: 6.83 us -> 13.4 us  [on_device(): piece = lax.ppermute(piece, EVERY, swap)]
    all_to_all x0 -> x1, starting transfers between devices: none -> 6.01 us  [on_device(): lax.all_to_all(copies, ROWS, split_axis=0, concat_axis=0, tiled=True)]
    reshape x2 -> x0, local copies, waits for them, and re-layouts: 2.71 us -> none  [as_output(): return rows.reshape(row_count, share, wide).transpose(1, 0, 2)]
  transfers between devices with their start and end apart: 4 -> 5, of which waited for: 4 -> 5; matrix products, arithmetic and copies ran while one was open for 1% -> 2% of each run, Pallas kernels for 0% -> 0%
where the time goes in v3:
time: 192 us; the launch traced here: 191 us
  blocking collectives  74.4 us (39%)
  waiting for transfers between devices  56.1 us (29%)
  starting transfers between devices  33.3 us (17%)
  Pallas kernels  18.8 us (10%)
  local copies, waits for them, and re-layouts  4.91 us (3%)
  other arithmetic  2.61 us (1%)
    all_to_all x2, blocking collectives, on_device(): lax.all_to_all(sent, 'hist', split_axis=0, concat_axis=0, tiled=True)  47.2 us
    ppermute x3, waiting for transfers between devices, on_device(): piece = lax.ppermute(piece, EVERY, swap)  32.9 us
    all_to_all x2, blocking collectives, on_device(): lax.all_to_all(copies, ROWS, split_axis=0, concat_axis=0, tiled=True)  27.3 us
    all_to_all x1, waiting for transfers between devices, on_device(): lax.all_to_all(sent, 'hist', split_axis=0, concat_axis=0, tiled=True)  14.5 us
    all_to_all x1, starting transfers between devices, on_device(): lax.all_to_all(sent, 'hist', split_axis=0, concat_axis=0, tiled=True)  13.9 us
    ppermute x3, starting transfers between devices, on_device(): piece = lax.ppermute(piece, EVERY, swap)  13.4 us
    pallas_call x3, Pallas kernels, on_device(): sent = contract(order, pieces, history)  11.6 us
    all_to_all x1, waiting for transfers between devices, on_device(): lax.all_to_all(copies, ROWS, split_axis=0, concat_axis=0, tiled=True)  8.76 us
  transfers between devices with their start and end apart: 5, of which 5 were waited for; matrix products, arithmetic and copies ran while one was open for 2% of the time, Pallas kernels for 0%

profile of v3, /device:TPU:32, one launch (start us, length us, event | category | flops | bytes accessed | tf_op | source)
XLA Modules:
  0.0 191.3 jit_solution(15635368386004149658)
XLA Ops:
  0.6 0.0 copy-start
  0.6 0.0 copy-start.2
  0.7 1.5 pad_maximum_fusion.coupling_ref
  2.2 0.7 pad_add_fusion.at_ref
  2.8 1.8 shard_map.86
  4.7 6.9 %collective-permute-start = (bf16[48,128]{1,0:T(8,128)(2,1)}, bf16[48,128]{1,0:T(8,128)(2,1)S(1)}, u32[]{:S(2)}, u32[]{:S(2)}) collective-permute-start(bf16[48,128]{1,0:T(8,128)(2,1)} %get-tuple-element.9), channel_id=1, source_target_pairs={{0,20},{1,21},{2,52},{3,53},{4,72},{5,73},{6,120},{7,121},{8,140},... | collective-permute-start | bytes 36872 | tf_op jit(solution)/shard_map/ppermute | solution.py:281
  11.6 10.3 %collective-permute-done = bf16[48,128]{1,0:T(8,128)(2,1)S(1)} collective-permute-done((bf16[48,128]{1,0:T(8,128)(2,1)}, bf16[48,128]{1,0:T(8,128)(2,1)S(1)}, u32[]{:S(2)}, u32[]{:S(2)}) %collective-permute-start) | collective-permute-done | bytes 12320 | tf_op jit(solution)/shard_map/ppermute | solution.py:281
  21.9 0.8 broadcast_in_dim.6
  22.7 6.0 %all-to-all-start = ((bf16[32,48,128]{2,1,0:T(8,128)(2,1)}), bf16[32,48,128]{2,1,0:T(8,128)(2,1)S(1)}, u32[]{:S(2)}, u32[]{:S(2)}) async-start(bf16[32,48,128]{2,1,0:T(8,128)(2,1)} %broadcast_in_dim.6), calls=%async_computation | async-start | bytes 786432 | tf_op jit(solution)/shard_map/all_to_all | solution.py:283
  28.7 1.2 fusion.10.order_ref
  29.9 8.8 %all-to-all-done.pieces_ref = bf16[32,48,128]{2,1,0:T(8,128)(2,1)S(1)} async-done(((bf16[32,48,128]{2,1,0:T(8,128)(2,1)}), bf16[32,48,128]{2,1,0:T(8,128)(2,1)S(1)}, u32[]{:S(2)}, u32[]{:S(2)}) %all-to-all-start) | async-done | bytes 393248 | tf_op jit(solution)/shard_map/all_to_all | solution.py:283
  38.7 0.0 copy-start.1
  38.7 0.8 copy-done.1
  39.5 3.9 %shard_map.87 = bf16[16,48,128]{2,1,0:T(8,128)(2,1)} custom-call(s32[16]{0:T(128)} %fusion.10.order_ref, bf16[32,48,128]{2,1,0:T(8,128)(2,1)} %copy-done.1, bf16[22,11,64,128]{3,2,1,0:T(8,128)(2,1)} %bitcast.38), custom_call_target="tpu_custom_call" | custom-call | tf_op jit(solution)/shard_map/pallas_call | solution.py:284
  43.3 13.9 %all-to-all-start.1 = ((bf16[16,48,128]{2,1,0:T(8,128)(2,1)}), bf16[16,48,128]{2,1,0:T(8,128)(2,1)S(1)}, u32[]{:S(2)}, u32[]{:S(2)}) async-start(bf16[16,48,128]{2,1,0:T(8,128)(2,1)} %shard_map.87), calls=%async_computation.1 | async-start | bytes 393216 | tf_op jit(solution)/shard_map/all_to_all | solution.py:285
  57.2 0.7 constant_dynamic-slice_fusion
  57.9 0.0 copy-done
  57.9 0.0 copy-done.2
  57.9 0.3 multiply_add_fusion
  58.2 0.4 fusion
  58.6 0.1 fusion.7
  58.7 0.1 maximum_bitcast_fusion
  58.8 0.6 pad.4.base_ref
  59.4 14.5 %all-to-all-done.1.arrived_ref = bf16[16,48,128]{2,1,0:T(8,128)(2,1)S(1)} async-done(((bf16[16,48,128]{2,1,0:T(8,128)(2,1)}), bf16[16,48,128]{2,1,0:T(8,128)(2,1)S(1)}, u32[]{:S(2)}, u32[]{:S(2)}) %all-to-all-start.1) | async-done | bytes 196640 | tf_op jit(solution)/shard_map/all_to_all | solution.py:285
  73.9 0.0 copy-start.3
  73.9 0.7 copy-done.3
  74.6 1.8 shard_map.88
  76.4 3.3 %collective-permute-start.1 = (bf16[48,128]{1,0:T(8,128)(2,1)}, bf16[48,128]{1,0:T(8,128)(2,1)S(1)}, u32[]{:S(2)}, u32[]{:S(2)}) collective-permute-start(bf16[48,128]{1,0:T(8,128)(2,1)} %shard_map.88), channel_id=1, source_target_pairs={{0,20},{1,21},{2,52},{3,53},{4,72},{5,73},{6,120},{7,121},{8,140},... | collective-permute-start | bytes 36872 | tf_op jit(solution)/shard_map/ppermute | solution.py:281
  79.7 11.2 %collective-permute-done.1 = bf16[48,128]{1,0:T(8,128)(2,1)S(1)} collective-permute-done((bf16[48,128]{1,0:T(8,128)(2,1)}, bf16[48,128]{1,0:T(8,128)(2,1)S(1)}, u32[]{:S(2)}, u32[]{:S(2)}) %collective-permute-start.1) | collective-permute-done | bytes 12320 | tf_op jit(solution)/shard_map/ppermute | solution.py:281
  91.0 0.1 broadcast_in_dim.7
  91.0 13.6 %all_to_all.30.pieces_ref = bf16[32,48,128]{2,1,0:T(8,128)(2,1)} all-to-all(bf16[32,48,128]{2,1,0:T(8,128)(2,1)S(1)} %broadcast_in_dim.7), channel_id=1, replica_groups=mesh['hist'=16,'rows_0'=4,'rows_1'=4,'rows_2'=2] {'rows_0','rows_1','row..., dimensions={0} | all-to-all | bytes 786432 | tf_op jit(solution)/shard_map/all_to_all | solution.py:283
  104.6 3.9 %shard_map.89 = bf16[16,48,128]{2,1,0:T(8,128)(2,1)} custom-call(s32[16]{0:T(128)} %fusion.10.order_ref, bf16[32,48,128]{2,1,0:T(8,128)(2,1)} %all_to_all.30.pieces_ref, bf16[22,11,64,128]{3,2,1,0:T(8,128)(2,1)} %bitcast.39), custom_call_target="tpu_custom_call" | custom-call | tf_op jit(solution)/shard_map/pallas_call | solution.py:284
  108.5 23.6 %all_to_all.31.arrived_ref = bf16[16,48,128]{2,1,0:T(8,128)(2,1)} all-to-all(bf16[16,48,128]{2,1,0:T(8,128)(2,1)} %shard_map.89), channel_id=1, replica_groups=mesh['hist'=16,'rows_0'=4,'rows_1'=4,'rows_2'=2] {'hist'}, dimensions={0} | all-to-all | bytes 393216 | tf_op jit(solution)/shard_map/all_to_all | solution.py:285
  132.1 1.9 shard_map.90
  134.0 3.2 %collective-permute-start.2 = (bf16[48,128]{1,0:T(8,128)(2,1)}, bf16[48,128]{1,0:T(8,128)(2,1)S(1)}, u32[]{:S(2)}, u32[]{:S(2)}) collective-permute-start(bf16[48,128]{1,0:T(8,128)(2,1)} %get-tuple-element.12), channel_id=1, source_target_pairs={{0,20},{1,21},{2,52},{3,53},{4,72},{5,73},{6,120},{7,121},{8,140},... | collective-permute-start | bytes 36872 | tf_op jit(solution)/shard_map/ppermute | solution.py:281
  137.1 11.3 %collective-permute-done.2 = bf16[48,128]{1,0:T(8,128)(2,1)S(1)} collective-permute-done((bf16[48,128]{1,0:T(8,128)(2,1)}, bf16[48,128]{1,0:T(8,128)(2,1)S(1)}, u32[]{:S(2)}, u32[]{:S(2)}) %collective-permute-start.2) | collective-permute-done | bytes 12320 | tf_op jit(solution)/shard_map/ppermute | solution.py:281
  148.5 0.1 broadcast_in_dim.8
  148.5 13.6 %all_to_all.32.pieces_ref = bf16[32,48,128]{2,1,0:T(8,128)(2,1)} all-to-all(bf16[32,48,128]{2,1,0:T(8,128)(2,1)S(1)} %broadcast_in_dim.8), channel_id=1, replica_groups=mesh['hist'=16,'rows_0'=4,'rows_1'=4,'rows_2'=2] {'rows_0','rows_1','row..., dimensions={0} | all-to-all | bytes 786432 | tf_op jit(solution)/shard_map/all_to_all | solution.py:283
  162.1 3.9 %shard_map.91 = bf16[16,48,128]{2,1,0:T(8,128)(2,1)} custom-call(s32[16]{0:T(128)} %fusion.10.order_ref, bf16[32,48,128]{2,1,0:T(8,128)(2,1)} %all_to_all.32.pieces_ref, bf16[22,11,64,128]{3,2,1,0:T(8,128)(2,1)} %bitcast.40), custom_call_target="tpu_custom_call" | custom-call | tf_op jit(solution)/shard_map/pallas_call | solution.py:284
  166.0 23.6 %all_to_all.33.arrived_ref = bf16[16,48,128]{2,1,0:T(8,128)(2,1)} all-to-all(bf16[16,48,128]{2,1,0:T(8,128)(2,1)} %shard_map.91), channel_id=1, replica_groups=mesh['hist'=16,'rows_0'=4,'rows_1'=4,'rows_2'=2] {'hist'}, dimensions={0} | all-to-all | bytes 393216 | tf_op jit(solution)/shard_map/all_to_all | solution.py:285
  189.6 1.7 shard_map.92
  (1 shorter events, 0.0 us)
Async XLA Ops:
  0.6 57.3 %copy-start = (f32[64,11,128]{2,0,1:T(8,128)S(1)}, f32[64,11,128]{2,0,1:T(8,128)}, u32[]{:S(2)}) copy-start(f32[64,11,128]{2,0,1:T(8,128)} %param.8) | copy-start | bytes 1081348
  0.6 57.3 %copy-start.2 = (f32[64,11,128]{2,0,1:T(8,128)S(1)}, f32[64,11,128]{2,0,1:T(8,128)}, u32[]{:S(2)}) copy-start(f32[64,11,128]{2,0,1:T(8,128)} %param.9) | copy-start | bytes 1081348
  4.7 17.2 %collective-permute-start = (bf16[48,128]{1,0:T(8,128)(2,1)}, bf16[48,128]{1,0:T(8,128)(2,1)S(1)}, u32[]{:S(2)}, u32[]{:S(2)}) collective-permute-start(bf16[48,128]{1,0:T(8,128)(2,1)} %get-tuple-element.9), channel_id=1, source_target_pairs={{0,20},{1,21},{2,52},{3,53},{4,72},{5,73},{6,120},{7,121},{8,140},... | collective-permute-start | bytes 36872 | tf_op jit(solution)/shard_map/ppermute | solution.py:281
  22.7 16.0 %all-to-all-start = ((bf16[32,48,128]{2,1,0:T(8,128)(2,1)}), bf16[32,48,128]{2,1,0:T(8,128)(2,1)S(1)}, u32[]{:S(2)}, u32[]{:S(2)}) async-start(bf16[32,48,128]{2,1,0:T(8,128)(2,1)} %broadcast_in_dim.6), calls=%async_computation | async-start | bytes 786432 | tf_op jit(solution)/shard_map/all_to_all | solution.py:283
  38.7 0.8 copy-start.1
  43.3 30.6 %all-to-all-start.1 = ((bf16[16,48,128]{2,1,0:T(8,128)(2,1)}), bf16[16,48,128]{2,1,0:T(8,128)(2,1)S(1)}, u32[]{:S(2)}, u32[]{:S(2)}) async-start(bf16[16,48,128]{2,1,0:T(8,128)(2,1)} %shard_map.87), calls=%async_computation.1 | async-start | bytes 393216 | tf_op jit(solution)/shard_map/all_to_all | solution.py:285
  73.9 0.7 copy-start.3
  76.4 14.5 %collective-permute-start.1 = (bf16[48,128]{1,0:T(8,128)(2,1)}, bf16[48,128]{1,0:T(8,128)(2,1)S(1)}, u32[]{:S(2)}, u32[]{:S(2)}) collective-permute-start(bf16[48,128]{1,0:T(8,128)(2,1)} %shard_map.88), channel_id=1, source_target_pairs={{0,20},{1,21},{2,52},{3,53},{4,72},{5,73},{6,120},{7,121},{8,140},... | collective-permute-start | bytes 36872 | tf_op jit(solution)/shard_map/ppermute | solution.py:281
  134.0 14.5 %collective-permute-start.2 = (bf16[48,128]{1,0:T(8,128)(2,1)}, bf16[48,128]{1,0:T(8,128)(2,1)S(1)}, u32[]{:S(2)}, u32[]{:S(2)}) collective-permute-start(bf16[48,128]{1,0:T(8,128)(2,1)} %get-tuple-element.12), channel_id=1, source_target_pairs={{0,20},{1,21},{2,52},{3,53},{4,72},{5,73},{6,120},{7,121},{8,140},... | collective-permute-start | bytes 36872 | tf_op jit(solution)/shard_map/ppermute | solution.py:281

commit v4 on v2

v4 whole, which is shorter than its diff:
```python
import functools

import jax
import jax.numpy as jnp
from jax import lax
from jax.experimental import pallas as pl
from jax.experimental.pallas import tpu as pltpu
from jax.sharding import Mesh
from jax.sharding import PartitionSpec as P

ITERS = 3
PLANE = ("rows_0", "rows_1")
ROWS = (*PLANE, "rows_2")
SMALL = 2.0**-90
LARGE = 2.0**90
FAR = 2.0**13

step_size = 0.5
half_step = 0.25


def halves(value):
    high = lax.reduce_precision(value, 8, 7)
    return high, lax.reduce_precision(value - high, 8, 7)


SCALARS = pl.BlockSpec(memory_space=pltpu.SMEM)
VECTORS = pl.BlockSpec(memory_space=pltpu.VMEM)


def call(kernel, shape, specs, scratch=()):
    outs = (VECTORS,) * len(shape) if isinstance(shape, tuple) else VECTORS
    return pl.pallas_call(
        kernel,
        out_shape=shape,
        in_specs=specs,
        out_specs=outs,
        scratch_shapes=list(scratch),
        compiler_params=pltpu.CompilerParams(vmem_limit_bytes=16 * 2**20),
    )


def low_half(shape):
    return lax.broadcasted_iota(jnp.int32, shape, len(shape) - 1) < shape[-1] // 2


def swapped(value):
    return pltpu.roll(value, value.shape[-1] // 2, axis=value.ndim - 1)


def notes(row, first, power, peak):
    high = power.astype(jnp.bfloat16).astype(jnp.float32)
    parts = (high, power - high, peak)
    value = jnp.zeros(row.shape, jnp.float32)
    for at, part in enumerate(parts):
        value = jnp.where(row == first + at, part, value)
    return value


def write_piece(piece_ref, field, factor_ref, mask_ref, damping, cells):
    row = lax.broadcasted_iota(jnp.int32, field.shape, 0)
    square = field * field
    square = square + swapped(square)
    power = jnp.sum(square * mask_ref[...], axis=(0, 1), keepdims=True)
    peak = jnp.max(jnp.where(row < cells, square, 0.0), axis=(0, 1), keepdims=True)
    sigma = factor_ref[...] * (square * damping) * field
    piece_ref[...] = jnp.where(row < cells, sigma, notes(row, cells, power, peak)).astype(
        piece_ref.dtype
    )


def packed(even, odd):
    even, odd = (value.reshape(-1, 8, value.shape[-1]) for value in (even, odd))
    upper = lax.broadcasted_iota(jnp.int32, even.shape, 1) < 4
    return (
        jnp.where(upper, even, pltpu.roll(odd, 4, axis=1)),
        jnp.where(upper, pltpu.roll(even, 4, axis=1), odd),
    )


def first_kernel(
    at_ref, rows_ref, coupling_ref, pieces_ref, factor_ref, mask_ref, terms_ref, *, share
):
    rows_at, plane_at, block_at = at_ref[0], at_ref[1], at_ref[2]
    times, orbits, wide = rows_ref.shape
    count, padded, _ = pieces_ref.shape
    row = lax.broadcasted_iota(jnp.int32, (orbits, wide), 0)
    lane = lax.broadcasted_iota(jnp.int32, (orbits, wide), 1)
    own = coupling_ref[...] * step_size
    power = jnp.zeros((orbits, wide), jnp.float32)
    peak = jnp.zeros((orbits, wide), jnp.float32)
    values = []
    for t in range(times):
        field = rows_ref[t]
        square = field * field
        square = square + swapped(square)
        power = power + jnp.where(lane == row, square, 0.0)
        peak = jnp.maximum(peak, square)
        scaled = jnp.where(rows_at == 0, own * 0.5, own) if t == 0 else own
        values.append(scaled * square * field)
    power = jnp.sum(power, axis=(0, 1), keepdims=True)
    peak = jnp.max(peak, axis=(0, 1), keepdims=True)
    values.append(notes(row % share, 0, jnp.where(row < share, power, 0.0), peak))
    for pair in range(padded // 8):
        terms_ref[:, 0, pair], terms_ref[:, 1, pair] = packed(*values[2 * pair : 2 * pair + 2])
    pieces_ref[...] = terms_ref[...].reshape(count, padded, wide).astype(pieces_ref.dtype)

    start = pl.multiple_of(plane_at // 2 * 8, 8)
    mine = coupling_ref[pl.ds(start, 8), :] * step_size
    turned = pltpu.roll(mine, 4, axis=0)
    row = lax.broadcasted_iota(jnp.int32, mine.shape, 0)
    lane = lax.broadcasted_iota(jnp.int32, mine.shape, 1)
    upper = row < share
    factor = jnp.where(upper == (plane_at % 2 == 0), mine, turned)
    mask = jnp.where(lane == plane_at * share + row % share, 1.0, 0.0)
    for group in range(padded // 8):
        scaled, kept = factor, mask
        if group == 0:
            scaled = jnp.where(upper & (block_at == 0), factor * 0.5, factor)
        if 2 * group + 1 == times:
            scaled, kept = jnp.where(upper, factor, 0.0), jnp.where(upper, mask, 0.0)
        factor_ref[8 * group : 8 * group + 8, :] = scaled
        mask_ref[8 * group : 8 * group + 8, :] = kept


def advance(arrived_ref, base_ref, restore, cells, total_cells):
    arrived = arrived_ref[:, : base_ref.shape[0]].astype(jnp.float32)
    total = jnp.sum(arrived, axis=0)
    row = lax.broadcasted_iota(jnp.int32, total.shape, 0)
    marked = (row == cells) | (row == cells + 1)
    power = jnp.sum(jnp.where(marked, total, 0.0), axis=0, keepdims=True)
    peak = jnp.max(jnp.where(row == cells + 2, jnp.max(arrived, axis=0), 0.0), axis=0, keepdims=True)
    integral = total / (1.0 + power / total_cells)
    if restore is not None:
        integral = integral * restore
    sign = jnp.where(low_half(total.shape), half_step, -half_step)
    return integral, base_ref[...] + swapped(integral) * sign, peak


def next_kernel(
    arrived_ref, factor_ref, mask_ref, piece_ref, base_ref, *, cells, total_cells
):
    count = arrived_ref.shape[0]
    padded, wide = base_ref.shape
    row = lax.broadcasted_iota(jnp.int32, (count, wide), 0)
    parts = padded // count
    gathered = [jnp.zeros((count, wide), jnp.float32) for _ in range(parts)]
    for h in range(count):
        extra = arrived_ref[h, padded:].astype(jnp.float32)
        for at in range(parts):
            value = extra[at : at + 1] + extra[parts + at : parts + at + 1]
            gathered[at] = jnp.where(row == h, value, gathered[at])
    base = jnp.concatenate(gathered, 0)
    row = lax.broadcasted_iota(jnp.int32, base.shape, 0)
    base_ref[...] = jnp.where(row < cells, base, 0.0)
    field = advance(arrived_ref, base_ref, None, cells, total_cells)[1]
    write_piece(piece_ref, field, factor_ref, mask_ref, 1.0, cells)


def guarded_kernel(
    arrived_ref, base_ref, factor_ref, mask_ref, piece_ref, restore_ref, *, cells, total_cells
):
    _, field, peak = advance(arrived_ref, base_ref, None, cells, total_cells)
    damping = jnp.where(peak > FAR, SMALL, 1.0)
    restore_ref[...] = jnp.broadcast_to(jnp.where(peak > FAR, LARGE, 1.0), restore_ref.shape)
    write_piece(piece_ref, field, factor_ref, mask_ref, damping, cells)


def last_kernel(arrived_ref, base_ref, restore_ref, row_ref, integral_ref, *, cells, total_cells):
    integral, field, _ = advance(arrived_ref, base_ref, restore_ref[0:1], cells, total_cells)
    times, share, _ = row_ref.shape
    for t in range(times):
        row_ref[t] = field[t * share : (t + 1) * share]
        integral_ref[t] = integral[t * share : (t + 1) * share]


def contract_kernel(pieces_ref, history_ref, *refs, times):
    *extra_refs, out_ref, field_ref, left_ref, terms_ref = refs
    count, padded, wide = pieces_ref.shape
    groups = padded // 8
    shares = count // 2
    orbits = wide // 2
    upper = lax.broadcasted_iota(jnp.int32, (groups, 8, wide), 1) < 4
    for k in range(2):
        for v in range(shares // 2):
            first = pieces_ref[4 * v + k].astype(jnp.float32).reshape(groups, 8, wide)
            second = pieces_ref[4 * v + 2 + k].astype(jnp.float32).reshape(groups, 8, wide)
            even = jnp.where(upper, first, pltpu.roll(second, 4, axis=1))
            odd = jnp.where(upper, pltpu.roll(first, 4, axis=1), second)
            field_ref[k, 0, :, 8 * v : 8 * v + 8, :] = even
            field_ref[k, 1, :, 8 * v : 8 * v + 8, :] = odd
    low = low_half((orbits, wide))
    for pair in range(times):
        blocks = []
        for s in (2 * pair, 2 * pair + 1):
            k, t = divmod(s, times)
            blocks.append(field_ref[k, t % 2, t // 2])
        lanes = slice(pair * wide, (pair + 1) * wide)
        left_ref[:orbits, lanes] = jnp.where(low, blocks[0], swapped(blocks[1])).astype(jnp.bfloat16)
        left_ref[orbits:, lanes] = jnp.where(low, swapped(blocks[0]), blocks[1]).astype(jnp.bfloat16)
    left = left_ref[...]
    depth = left.shape[1]
    sign = jnp.where(low, -1.0, 1.0)
    which = lax.broadcasted_iota(jnp.int32, (orbits, wide), 0) % 4
    marks = [field_ref[k, 1, groups - 1] for k in range(2)]
    power = jnp.sum(jnp.where(which < 2, marks[0] + marks[1], 0.0), axis=0, keepdims=True)
    peak = jnp.max(
        jnp.where(which == 2, jnp.maximum(marks[0], marks[1]), 0.0), axis=0, keepdims=True
    )
    for pair in range(groups):
        moments = [t for t in (2 * pair, 2 * pair + 1) if t < times]
        right = [history_ref[:, t].reshape(depth, wide) for t in moments]
        right = jnp.concatenate(right, -1) if len(right) > 1 else right[0]
        product = jnp.dot(left, right, preferred_element_type=jnp.float32)
        values = []
        for at in range(len(moments)):
            lanes = slice(at * wide, (at + 1) * wide)
            values.append(product[:orbits, lanes] + swapped(product[orbits:, lanes]) * sign)
        if len(moments) < 2:
            values.append(notes(which, 0, power, peak))
        terms_ref[:, 0, pair], terms_ref[:, 1, pair] = packed(*values)
    out_ref[:, :padded] = terms_ref[...].reshape(shares, padded, wide).astype(out_ref.dtype)
    for extra_ref in extra_refs:
        out_ref[:, padded:] = extra_ref[...]


def on_device(g_hist, g_last, integral_last, coupling, step_re, step_im):
    orbits = g_last.shape[0]
    row_count = g_last.shape[1]
    wide = 2 * orbits
    hist_size = lax.axis_size("hist")
    rows_size = lax.axis_size(ROWS)
    fan_out = rows_size // hist_size
    hist_at = lax.axis_index("hist")
    rows_at = lax.axis_index(ROWS)
    plane_at = lax.axis_index(PLANE)
    core_at = lax.axis_index(ROWS[-1])
    total_cells = row_count * rows_size * orbits
    share = orbits // hist_size
    cells = share * row_count
    padded = cells + share
    def exchange(blocks, axes):
        return lax.all_to_all(blocks, axes, split_axis=0, concat_axis=0, tiled=True)

    def my_rows(whole):
        return lax.dynamic_slice_in_dim(whole, hist_at * share, share, 0)

    def as_rows(value):
        value = value.transpose(1, 0, 2).reshape(cells, wide)
        return jnp.pad(value, ((0, padded - cells), (0, 0)))

    def stepped(steps_re, steps_im, rows, integrals):
        shifted = jnp.concatenate(
            [
                rows[..., :orbits] + half_step * integrals[..., orbits:],
                rows[..., orbits:] - half_step * integrals[..., :orbits],
            ],
            -1,
        )
        moved = lax.dot_general(
            jnp.concatenate([steps_re, steps_im], 0),
            shifted,
            (((1,), (1,)), ((), ())),
            precision=lax.Precision.HIGHEST,
            preferred_element_type=jnp.float32,
        ).reshape(2, steps_re.shape[0], rows.shape[0], wide)
        return jnp.concatenate(
            [
                moved[0, ..., :orbits] - moved[1, ..., orbits:],
                moved[0, ..., orbits:] + moved[1, ..., :orbits],
            ],
            -1,
        )

    def base_rows(integral_last):
        by_time = (value.transpose(1, 0, 2) for value in (g_last, integral_last))
        return as_rows(stepped(my_rows(step_re), my_rows(step_im), *by_time))

    def base_chunk():
        def rows_like(steps):
            steps = steps.reshape(hist_size, share, orbits)
            return lax.dynamic_index_in_dim(steps, hist_at % share, 1, keepdims=False)

        def some_times(value):
            value = value.transpose(1, 0, 2)
            start = hist_at // share
            stride = hist_size // share
            return jnp.concatenate(
                [
                    lax.dynamic_slice_in_dim(value, jnp.minimum(start + t, row_count - 1), 1, 0)
                    for t in range(0, padded // share, stride)
                ],
                0,
            )

        chunk = stepped(
            rows_like(step_re), rows_like(step_im), some_times(g_last), some_times(integral_last)
        )
        parts = jnp.concatenate(halves(chunk), 1).astype(jnp.bfloat16)
        return jnp.pad(parts, ((0, 0), (0, hist_size - parts.shape[1]), (0, 0)))

    history = g_hist.transpose(0, 2, 1, 3)
    piece_shape = jax.ShapeDtypeStruct((padded, wide), jnp.bfloat16)
    local_shape = jax.ShapeDtypeStruct((padded, wide), jnp.float32)
    row_shape = jax.ShapeDtypeStruct((row_count, share, wide), jnp.float32)
    sizes = {"cells": cells, "total_cells": total_cells}
    pieces_shape = jax.ShapeDtypeStruct((hist_size, padded, wide), jnp.bfloat16)
    terms = pltpu.VMEM((hist_size // 2, 2, padded // 8, 8, wide), jnp.float32)
    spread, factor, mask = call(
        functools.partial(first_kernel, share=share),
        (pieces_shape, local_shape, local_shape),
        (SCALARS, VECTORS, VECTORS),
        [terms],
    )(
        jnp.stack([rows_at, plane_at, hist_at * fan_out + core_at]).astype(jnp.int32),
        g_last.transpose(1, 0, 2),
        jnp.concatenate([coupling, coupling], -1),
    )
    def contract(pieces, *extra):
        rows = padded + sum(value.shape[1] for value in extra)
        return call(
            functools.partial(contract_kernel, times=row_count),
            jax.ShapeDtypeStruct((hist_size, rows, wide), jnp.bfloat16),
            (VECTORS,) * (2 + len(extra)),
            [
                pltpu.VMEM((fan_out, 2, padded // 8, orbits, wide), jnp.float32),
                pltpu.VMEM((wide, fan_out * row_count * orbits), jnp.bfloat16),
                terms,
            ],
        )(pieces, history, *extra)

    piece = lax.dynamic_index_in_dim(exchange(spread, PLANE), hist_at, 0, keepdims=False)
    for iteration in range(ITERS):
        copies = jnp.broadcast_to(piece[None], (rows_size, padded, wide))
        extra = (base_chunk(),) if iteration == 0 else ()
        sent = contract(exchange(copies, ROWS), *extra)
        if iteration == 0:
            integral_held, sent = lax.optimization_barrier((integral_last, sent))
            base = base_rows(integral_held)
        if iteration < ITERS - 1:
            sent = exchange(sent, PLANE)
        arrived = exchange(sent, "hist")
        if iteration == 0:
            piece, base_moved = call(
                functools.partial(next_kernel, **sizes), (piece_shape, local_shape), (VECTORS,) * 3
            )(arrived, factor, mask)
        elif iteration == 1:
            piece, restore = call(
                functools.partial(guarded_kernel, **sizes),
                (piece_shape, jax.ShapeDtypeStruct((8, wide), jnp.float32)),
                (VECTORS,) * 4,
            )(arrived, base_moved, factor, mask)
        else:
            new_row, new_integral = call(
                functools.partial(last_kernel, **sizes), (row_shape, row_shape), (VECTORS,) * 3
            )(arrived, base, restore)
    return new_row.transpose(1, 0, 2), new_integral.transpose(1, 0, 2)


def solution(mesh):
    split = Mesh(
        mesh.devices.reshape(mesh.shape["hist"], 4, 4, 2), ("hist", "rows_0", "rows_1", "rows_2")
    )
    return jax.shard_map(
        on_device,
        mesh=split,
        in_specs=(
            P("hist", None, ROWS, None),
            P(None, ROWS, None),
            P(None, ROWS, None),
            P(),
            P(),
            P(),
        ),
        out_specs=(P("hist", ROWS, None), P("hist", ROWS, None)),
        check_vma=False,
    )
```

time: 198 us -> 172 us (0.87)
  blocking collectives: 121 us -> 91.7 us
  waiting for transfers between devices: 27.8 us -> 40 us
  Pallas kernels: 18.5 us -> 6.31 us
  local copies, waits for them, and re-layouts: 7.79 us -> 10.1 us
    all_to_all x5, blocking collectives: 121 us -> 91.7 us  [exchange(): return lax.all_to_all(blocks, axes, split_axis=0, concat_axis=0, tiled=True)]
    all_to_all x1 -> x4, waiting for transfers between devices: 14.5 us -> 40 us  [exchange(): return lax.all_to_all(blocks, axes, split_axis=0, concat_axis=0, tiled=True)]
    ppermute x3 -> x0, waiting for transfers between devices: 13.3 us -> none  [on_device(): piece = lax.ppermute(piece, EVERY, swap)]
    pallas_call x7, Pallas kernels: 18.5 us -> 6.31 us  [the longest x3 3.46 us: contract(): call(functools.partial(contract_kernel, times=row_count), jax.ShapeDtypeS...]
    all_to_all x1 -> x4, starting transfers between devices: 12.9 us -> 19.9 us  [exchange(): return lax.all_to_all(blocks, axes, split_axis=0, concat_axis=0, tiled=True)]
    ppermute x3 -> x0, starting transfers between devices: 6.83 us -> none  [on_device(): piece = lax.ppermute(piece, EVERY, swap)]
    unnamed x8 -> x12, local copies, waits for them, and re-layouts: 1.39 us -> 5.25 us
    reshape x2 -> x0, local copies, waits for them, and re-layouts: 2.71 us -> none  [as_output(): return rows.reshape(row_count, share, wide).transpose(1, 0, 2)]
  transfers between devices with their start and end apart: 4 -> 4, of which waited for: 4 -> 4; matrix products, arithmetic and copies ran while one was open for 1% -> 3% of each run, Pallas kernels for 0% -> 0%
where the time goes in v4:
time: 172 us; the launch traced here: 171 us
  blocking collectives  91.7 us (53%)
  waiting for transfers between devices  40 us (23%)
  starting transfers between devices  19.9 us (12%)
  local copies, waits for them, and re-layouts  10.1 us (6%)
  Pallas kernels  6.31 us (4%)
  other arithmetic  1.76 us (1%)
    all_to_all x5, blocking collectives, exchange(): return lax.all_to_all(blocks, axes, split_axis=0, concat_axis=0, tiled=True)  91.7 us
    all_to_all x4, waiting for transfers between devices, exchange(): return lax.all_to_all(blocks, axes, split_axis=0, concat_axis=0, tiled=True)  40 us
    all_to_all x4, starting transfers between devices, exchange(): return lax.all_to_all(blocks, axes, split_axis=0, concat_axis=0, tiled=True)  19.9 us
    unnamed x12, local copies, waits for them, and re-layouts  5.25 us
    pallas_call x3, Pallas kernels, contract(): call(functools.partial(contract_kernel, times=row_count), jax.ShapeDtypeS...  3.46 us
  transfers between devices with their start and end apart: 4, of which 4 were waited for; matrix products, arithmetic and copies ran while one was open for 3% of the time, Pallas kernels for 0%

profile of v4, /device:TPU:32, one launch (start us, length us, event | category | flops | bytes accessed | tf_op | source)
XLA Modules:
  0.0 171.4 jit_solution(12501282854888589642)
XLA Ops:
  0.6 0.9 pad_maximum_fusion.2.coupling_ref
  1.6 0.1 pad_add_fusion.at_ref
  1.6 0.0 copy-start.3
  1.6 1.0 copy-done.3
  2.6 1.5 shard_map.77
  4.1 7.0 %all-to-all-start = ((bf16[16,48,128]{2,1,0:T(8,128)(2,1)}), bf16[16,48,128]{2,1,0:T(8,128)(2,1)S(1)}, u32[]{:S(2)}, u32[]{:S(2)}) async-start(bf16[16,48,128]{2,1,0:T(8,128)(2,1)} %get-tuple-element.13), calls=%async_computation | async-start | bytes 393216 | tf_op jit(solution)/shard_map/all_to_all | solution.py:243
  11.2 0.8 dynamic-slice_bitcast_fusion.5
  12.0 0.8 dynamic-slice_bitcast_fusion.2
  12.8 0.1 fusion.9
  13.0 0.8 constant_dynamic-slice_fusion.2
  13.8 0.3 fusion.10
  14.1 5.3 %all-to-all-done = bf16[16,48,128]{2,1,0:T(8,128)(2,1)S(1)} async-done(((bf16[16,48,128]{2,1,0:T(8,128)(2,1)}), bf16[16,48,128]{2,1,0:T(8,128)(2,1)S(1)}, u32[]{:S(2)}, u32[]{:S(2)}) %all-to-all-start) | async-done | bytes 196640 | tf_op jit(solution)/shard_map/all_to_all | solution.py:243
  19.4 0.8 broadcast_in_dim.9
  20.2 3.9 %all-to-all-start.1 = ((bf16[32,48,128]{2,1,0:T(8,128)(2,1)}), bf16[32,48,128]{2,1,0:T(8,128)(2,1)S(1)}, u32[]{:S(2)}, u32[]{:S(2)}) async-start(bf16[32,48,128]{2,1,0:T(8,128)(2,1)} %broadcast_in_dim.9), calls=%async_computation.1 | async-start | bytes 786432 | tf_op jit(solution)/shard_map/all_to_all | solution.py:243
  24.1 0.1 fusion.18
  24.2 0.1 reduce-precision_convert_fusion
  24.3 9.7 %all-to-all-done.1.pieces_ref = bf16[32,48,128]{2,1,0:T(8,128)(2,1)S(1)} async-done(((bf16[32,48,128]{2,1,0:T(8,128)(2,1)}), bf16[32,48,128]{2,1,0:T(8,128)(2,1)S(1)}, u32[]{:S(2)}, u32[]{:S(2)}) %all-to-all-start.1) | async-done | bytes 393248 | tf_op jit(solution)/shard_map/all_to_all | solution.py:243
  34.0 0.0 copy-start
  34.0 2.1 %copy-done = bf16[22,64,11,128]{3,1,2,0:T(8,128)(2,1)S(1)} copy-done((bf16[22,64,11,128]{3,1,2,0:T(8,128)(2,1)S(1)}, bf16[22,64,11,128]{3,1,2,0:T(8,128)(2,1)}, u32[]{:S(2)}) %copy-start) | copy-done | bytes 3964952
  36.2 0.0 copy-start.1
  36.2 0.9 shard_map.78
  37.1 12.5 %all_to_all.45 = bf16[16,64,128]{2,1,0:T(8,128)(2,1)S(1)} all-to-all(bf16[16,64,128]{2,1,0:T(8,128)(2,1)S(1)} %shard_map.78), channel_id=1, replica_groups=mesh['hist'=16,'rows_0'=4,'rows_1'=4,'rows_2'=2] {'rows_0','rows_1'}, dimensions={0} | all-to-all | bytes 524288 | tf_op jit(solution)/shard_map/all_to_all | solution.py:243
  49.6 32.8 %all_to_all.46.arrived_ref = bf16[16,64,128]{2,1,0:T(8,128)(2,1)S(1)} all-to-all(bf16[16,64,128]{2,1,0:T(8,128)(2,1)S(1)} %all_to_all.45), channel_id=1, replica_groups=mesh['hist'=16,'rows_0'=4,'rows_1'=4,'rows_2'=2] {'hist'}, dimensions={0} | all-to-all | bytes 524288 | tf_op jit(solution)/shard_map/all_to_all | solution.py:243
  82.3 0.3 shard_map.79
  82.7 0.1 broadcast_in_dim.10
  82.7 13.5 %all_to_all.47.pieces_ref = bf16[32,48,128]{2,1,0:T(8,128)(2,1)S(1)} all-to-all(bf16[32,48,128]{2,1,0:T(8,128)(2,1)S(1)} %broadcast_in_dim.10), channel_id=1, replica_groups=mesh['hist'=16,'rows_0'=4,'rows_1'=4,'rows_2'=2] {'rows_0','rows_1','row..., dimensions={0} | all-to-all | bytes 786432 | tf_op jit(solution)/shard_map/all_to_all | solution.py:243
  96.2 0.0 copy-done.1
  96.2 0.9 shard_map.80
  97.1 0.0 copy-start.4
  97.1 0.0 copy-start.5
  97.1 11.8 %all_to_all.48 = bf16[16,48,128]{2,1,0:T(8,128)(2,1)S(1)} all-to-all(bf16[16,48,128]{2,1,0:T(8,128)(2,1)S(1)} %shard_map.80), channel_id=1, replica_groups=mesh['hist'=16,'rows_0'=4,'rows_1'=4,'rows_2'=2] {'rows_0','rows_1'}, dimensions={0} | all-to-all | bytes 393216 | tf_op jit(solution)/shard_map/all_to_all | solution.py:243
  109.0 21.2 %all_to_all.49.arrived_ref = bf16[16,48,128]{2,1,0:T(8,128)(2,1)S(1)} all-to-all(bf16[16,48,128]{2,1,0:T(8,128)(2,1)S(1)} %all_to_all.48), channel_id=1, replica_groups=mesh['hist'=16,'rows_0'=4,'rows_1'=4,'rows_2'=2] {'hist'}, dimensions={0} | all-to-all | bytes 393216 | tf_op jit(solution)/shard_map/all_to_all | solution.py:243
  130.1 0.3 shard_map.81
  130.4 0.8 broadcast_in_dim.11
  131.2 4.4 %all-to-all-start.7 = ((bf16[32,48,128]{2,1,0:T(8,128)(2,1)}), bf16[32,48,128]{2,1,0:T(8,128)(2,1)S(1)}, u32[]{:S(2)}, u32[]{:S(2)}) async-start(bf16[32,48,128]{2,1,0:T(8,128)(2,1)} %broadcast_in_dim.11), calls=%async_computation.7 | async-start | bytes 786432 | tf_op jit(solution)/shard_map/all_to_all | solution.py:243
  135.7 10.0 %all-to-all-done.7.pieces_ref = bf16[32,48,128]{2,1,0:T(8,128)(2,1)S(1)} async-done(((bf16[32,48,128]{2,1,0:T(8,128)(2,1)}), bf16[32,48,128]{2,1,0:T(8,128)(2,1)S(1)}, u32[]{:S(2)}, u32[]{:S(2)}) %all-to-all-start.7) | async-done | bytes 393248 | tf_op jit(solution)/shard_map/all_to_all | solution.py:243
  145.6 0.0 copy-start.2
  145.6 2.1 %copy-done.2 = bf16[22,64,11,128]{3,1,2,0:T(8,128)(2,1)S(1)} copy-done((bf16[22,64,11,128]{3,1,2,0:T(8,128)(2,1)S(1)}, bf16[22,64,11,128]{3,1,2,0:T(8,128)(2,1)}, u32[]{:S(2)}) %copy-start.2) | copy-done | bytes 3964952
  147.7 1.6 shard_map.82
  149.3 4.6 %all-to-all-start.8 = ((bf16[16,48,128]{2,1,0:T(8,128)(2,1)}), bf16[16,48,128]{2,1,0:T(8,128)(2,1)S(1)}, u32[]{:S(2)}, u32[]{:S(2)}) async-start(bf16[16,48,128]{2,1,0:T(8,128)(2,1)} %shard_map.82), calls=%async_computation.8 | async-start | bytes 393216 | tf_op jit(solution)/shard_map/all_to_all | solution.py:243
  154.0 0.7 constant_dynamic-slice_fusion
  154.7 0.0 copy-done.4
  154.7 0.0 copy-done.5
  154.7 0.3 fusion.1
  154.9 0.4 fusion.2
  155.3 0.1 fusion.22
  155.4 0.1 maximum_bitcast_fusion
  155.5 15.1 %all-to-all-done.8.arrived_ref = bf16[16,48,128]{2,1,0:T(8,128)(2,1)S(1)} async-done(((bf16[16,48,128]{2,1,0:T(8,128)(2,1)}), bf16[16,48,128]{2,1,0:T(8,128)(2,1)S(1)}, u32[]{:S(2)}, u32[]{:S(2)}) %all-to-all-start.8) | async-done | bytes 196640 | tf_op jit(solution)/shard_map/all_to_all | solution.py:243
  170.6 0.7 shard_map.83
  (6 shorter events, 0.1 us)
Async XLA Ops:
  1.6 1.0 copy-start.3
  4.1 15.2 %all-to-all-start = ((bf16[16,48,128]{2,1,0:T(8,128)(2,1)}), bf16[16,48,128]{2,1,0:T(8,128)(2,1)S(1)}, u32[]{:S(2)}, u32[]{:S(2)}) async-start(bf16[16,48,128]{2,1,0:T(8,128)(2,1)} %get-tuple-element.13), calls=%async_computation | async-start | bytes 393216 | tf_op jit(solution)/shard_map/all_to_all | solution.py:243
  20.2 13.9 %all-to-all-start.1 = ((bf16[32,48,128]{2,1,0:T(8,128)(2,1)}), bf16[32,48,128]{2,1,0:T(8,128)(2,1)S(1)}, u32[]{:S(2)}, u32[]{:S(2)}) async-start(bf16[32,48,128]{2,1,0:T(8,128)(2,1)} %broadcast_in_dim.9), calls=%async_computation.1 | async-start | bytes 786432 | tf_op jit(solution)/shard_map/all_to_all | solution.py:243
  34.0 2.1 %copy-start = (bf16[22,64,11,128]{3,1,2,0:T(8,128)(2,1)S(1)}, bf16[22,64,11,128]{3,1,2,0:T(8,128)(2,1)}, u32[]{:S(2)}) copy-start(bf16[22,64,11,128]{3,1,2,0:T(8,128)(2,1)} %param.6) | copy-start | bytes 11894788
  36.2 60.0 %copy-start.1 = (bf16[22,64,11,128]{3,1,2,0:T(8,128)(2,1)S(1)}, bf16[22,64,11,128]{3,1,2,0:T(8,128)(2,1)}, u32[]{:S(2)}) copy-start(bf16[22,64,11,128]{3,1,2,0:T(8,128)(2,1)} %param.6) | copy-start | bytes 11894788
  97.1 57.5 %copy-start.4 = (f32[64,11,128]{2,0,1:T(8,128)S(1)}, f32[64,11,128]{2,0,1:T(8,128)}, u32[]{:S(2)}) copy-start(f32[64,11,128]{2,0,1:T(8,128)} %param.7) | copy-start | bytes 1081348
  97.1 57.5 %copy-start.5 = (f32[64,11,128]{2,0,1:T(8,128)S(1)}, f32[64,11,128]{2,0,1:T(8,128)}, u32[]{:S(2)}) copy-start(f32[64,11,128]{2,0,1:T(8,128)} %param.8) | copy-start | bytes 1081348
  131.2 14.4 %all-to-all-start.7 = ((bf16[32,48,128]{2,1,0:T(8,128)(2,1)}), bf16[32,48,128]{2,1,0:T(8,128)(2,1)S(1)}, u32[]{:S(2)}, u32[]{:S(2)}) async-start(bf16[32,48,128]{2,1,0:T(8,128)(2,1)} %broadcast_in_dim.11), calls=%async_computation.7 | async-start | bytes 786432 | tf_op jit(solution)/shard_map/all_to_all | solution.py:243
  145.6 2.1 %copy-start.2 = (bf16[22,64,11,128]{3,1,2,0:T(8,128)(2,1)S(1)}, bf16[22,64,11,128]{3,1,2,0:T(8,128)(2,1)}, u32[]{:S(2)}) copy-start(bf16[22,64,11,128]{3,1,2,0:T(8,128)(2,1)} %param.6) | copy-start | bytes 11894788
  149.3 21.3 %all-to-all-start.8 = ((bf16[16,48,128]{2,1,0:T(8,128)(2,1)}), bf16[16,48,128]{2,1,0:T(8,128)(2,1)S(1)}, u32[]{:S(2)}, u32[]{:S(2)}) async-start(bf16[16,48,128]{2,1,0:T(8,128)(2,1)} %shard_map.82), calls=%async_computation.8 | async-start | bytes 393216 | tf_op jit(solution)/shard_map/all_to_all | solution.py:243

commit v5 on v4

--- a/solution.py
+++ b/solution.py
@@ -14,18 +14,15 @@
 SMALL = 2.0**-90
 LARGE = 2.0**90
 FAR = 2.0**13
+SMALL_VMEM = 16 * 2**20
 
 step_size = 0.5
 half_step = 0.25
 
 
-def halves(value):
-    high = lax.reduce_precision(value, 8, 7)
-    return high, lax.reduce_precision(value - high, 8, 7)
-
-
 SCALARS = pl.BlockSpec(memory_space=pltpu.SMEM)
 VECTORS = pl.BlockSpec(memory_space=pltpu.VMEM)
+OUTSIDE = pl.BlockSpec(memory_space=pltpu.HBM)
 
 
 def call(kernel, shape, specs, scratch=()):
@@ -36,7 +33,7 @@
         in_specs=specs,
         out_specs=outs,
         scratch_shapes=list(scratch),
-        compiler_params=pltpu.CompilerParams(vmem_limit_bytes=16 * 2**20),
+        compiler_params=pltpu.CompilerParams(vmem_limit_bytes=None if OUTSIDE in specs else SMALL_VMEM),
     )
 
 
@@ -69,6 +66,17 @@
     )
 
 
+def fetch(sources, held, sems):
+    copies = [
+        pltpu.make_async_copy(source, target, sems.at[at])
+        for at, (source, target) in enumerate(zip(sources, held))
+    ]
+    for copy in copies:
+        copy.start()
+    for copy in copies:
+        copy.wait()
+
+
 def packed(even, odd):
     even, odd = (value.reshape(-1, 8, value.shape[-1]) for value in (even, odd))
     upper = lax.broadcasted_iota(jnp.int32, even.shape, 1) < 4
@@ -78,15 +86,17 @@
     )
 
 
-def first_kernel(
-    at_ref, rows_ref, coupling_ref, pieces_ref, factor_ref, mask_ref, terms_ref, *, share
-):
+def first_kernel(at_ref, *refs, share):
+    pieces_ref, factor_ref, mask_ref, terms_ref = refs[2:6]
+    rows_ref, coupling_ref = refs[6:8]
+    fetch(refs[:2], refs[6:8], refs[8])
     rows_at, plane_at, block_at = at_ref[0], at_ref[1], at_ref[2]
     times, orbits, wide = rows_ref.shape
     count, padded, _ = pieces_ref.shape
     row = lax.broadcasted_iota(jnp.int32, (orbits, wide), 0)
     lane = lax.broadcasted_iota(jnp.int32, (orbits, wide), 1)
     own = coupling_ref[...] * step_size
+    own = jnp.concatenate([own, own], -1)
     power = jnp.zeros((orbits, wide), jnp.float32)
     peak = jnp.zeros((orbits, wide), jnp.float32)
     values = []
@@ -107,6 +117,7 @@
 
     start = pl.multiple_of(plane_at // 2 * 8, 8)
     mine = coupling_ref[pl.ds(start, 8), :] * step_size
+    mine = jnp.concatenate([mine, mine], -1)
     turned = pltpu.roll(mine, 4, axis=0)
     row = lax.broadcasted_iota(jnp.int32, mine.shape, 0)
     lane = lax.broadcasted_iota(jnp.int32, mine.shape, 1)
@@ -121,6 +132,47 @@
             scaled, kept = jnp.where(upper, factor, 0.0), jnp.where(upper, mask, 0.0)
         factor_ref[8 * group : 8 * group + 8, :] = scaled
         mask_ref[8 * group : 8 * group + 8, :] = kept
+
+
+def base_kernel(at_ref, *refs):
+    base_ref, extra_ref, terms_ref = refs[4:7]
+    rows_ref, integrals_ref, step_re_ref, step_im_ref = refs[7:11]
+    fetch(refs[:4], refs[7:11], refs[11])
+    hist_at = at_ref[0]
+    times, orbits, wide = rows_ref.shape
+    count = extra_ref.shape[0]
+    padded = base_ref.shape[0]
+    low = low_half((orbits, wide))
+    sign = jnp.where(low, half_step, -half_step)
+    turn = jnp.where(low, -1.0, 1.0)
+    shifted = [rows_ref[t] + swapped(integrals_ref[t]) * sign for t in range(times)]
+    steps = jnp.concatenate([step_re_ref[...], step_im_ref[...]], 0)
+    moved = jnp.dot(
+        steps,
+        jnp.concatenate(shifted, -1),
+        precision=lax.Precision.HIGHEST,
+        preferred_element_type=jnp.float32,
+    )
+    values = []
+    for t in range(times):
+        lanes = slice(t * wide, (t + 1) * wide)
+        values.append(moved[:orbits, lanes] + swapped(moved[orbits:, lanes]) * turn)
+    values.append(jnp.zeros((orbits, wide), jnp.float32))
+    for pair in range(padded // 8):
+        terms_ref[:, 0, pair], terms_ref[:, 1, pair] = packed(*values[2 * pair : 2 * pair + 2])
+    base_ref[...] = terms_ref[hist_at // 2, hist_at % 2].reshape(padded, wide)
+    parts = padded // count
+    sub = lax.broadcasted_iota(jnp.int32, (8, wide), 0)
+    row = lax.broadcasted_iota(jnp.int32, extra_ref.shape[1:], 0)
+    for share in range(count):
+        extra = jnp.zeros(row.shape, jnp.float32)
+        for at in range(parts):
+            group = terms_ref[share // 2, share % 2, at * (count // 8) + hist_at // 8]
+            value = jnp.sum(jnp.where(sub == hist_at % 8, group, 0.0), axis=0, keepdims=True)
+            high = value.astype(jnp.bfloat16).astype(jnp.float32)
+            extra = jnp.where(row == at, high, extra)
+            extra = jnp.where(row == parts + at, value - high, extra)
+        extra_ref[share] = extra.astype(extra_ref.dtype)
 
 
 def advance(arrived_ref, base_ref, restore, cells, total_cells):
@@ -242,63 +294,6 @@
     def exchange(blocks, axes):
         return lax.all_to_all(blocks, axes, split_axis=0, concat_axis=0, tiled=True)
 
-    def my_rows(whole):
-        return lax.dynamic_slice_in_dim(whole, hist_at * share, share, 0)
-
-    def as_rows(value):
-        value = value.transpose(1, 0, 2).reshape(cells, wide)
-        return jnp.pad(value, ((0, padded - cells), (0, 0)))
-
-    def stepped(steps_re, steps_im, rows, integrals):
-        shifted = jnp.concatenate(
-            [
-                rows[..., :orbits] + half_step * integrals[..., orbits:],
-                rows[..., orbits:] - half_step * integrals[..., :orbits],
-            ],
-            -1,
-        )
-        moved = lax.dot_general(
-            jnp.concatenate([steps_re, steps_im], 0),
-            shifted,
-            (((1,), (1,)), ((), ())),
-            precision=lax.Precision.HIGHEST,
-            preferred_element_type=jnp.float32,
-        ).reshape(2, steps_re.shape[0], rows.shape[0], wide)
-        return jnp.concatenate(
-            [
-                moved[0, ..., :orbits] - moved[1, ..., orbits:],
-                moved[0, ..., orbits:] + moved[1, ..., :orbits],
-            ],
-            -1,
-        )
-
-    def base_rows(integral_last):
-        by_time = (value.transpose(1, 0, 2) for value in (g_last, integral_last))
-        return as_rows(stepped(my_rows(step_re), my_rows(step_im), *by_time))
-
-    def base_chunk():
-        def rows_like(steps):
-            steps = steps.reshape(hist_size, share, orbits)
-            return lax.dynamic_index_in_dim(steps, hist_at % share, 1, keepdims=False)
-
-        def some_times(value):
-            value = value.transpose(1, 0, 2)
-            start = hist_at // share
-            stride = hist_size // share
-            return jnp.concatenate(
-                [
-                    lax.dynamic_slice_in_dim(value, jnp.minimum(start + t, row_count - 1), 1, 0)
-                    for t in range(0, padded // share, stride)
-                ],
-                0,
-            )
-
-        chunk = stepped(
-            rows_like(step_re), rows_like(step_im), some_times(g_last), some_times(integral_last)
-        )
-        parts = jnp.concatenate(halves(chunk), 1).astype(jnp.bfloat16)
-        return jnp.pad(parts, ((0, 0), (0, hist_size - parts.shape[1]), (0, 0)))
-
     history = g_hist.transpose(0, 2, 1, 3)
     piece_shape = jax.ShapeDtypeStruct((padded, wide), jnp.bfloat16)
     local_shape = jax.ShapeDtypeStruct((padded, wide), jnp.float32)
@@ -306,16 +301,32 @@
     sizes = {"cells": cells, "total_cells": total_cells}
     pieces_shape = jax.ShapeDtypeStruct((hist_size, padded, wide), jnp.bfloat16)
     terms = pltpu.VMEM((hist_size // 2, 2, padded // 8, 8, wide), jnp.float32)
+    by_time = [pltpu.VMEM((row_count, orbits, wide), jnp.float32)] * 2
+    square = pltpu.VMEM((orbits, orbits), jnp.float32)
     spread, factor, mask = call(
         functools.partial(first_kernel, share=share),
         (pieces_shape, local_shape, local_shape),
-        (SCALARS, VECTORS, VECTORS),
-        [terms],
+        (SCALARS, OUTSIDE, OUTSIDE),
+        [terms, *by_time[:1], square, pltpu.SemaphoreType.DMA((2,))],
     )(
         jnp.stack([rows_at, plane_at, hist_at * fan_out + core_at]).astype(jnp.int32),
         g_last.transpose(1, 0, 2),
-        jnp.concatenate([coupling, coupling], -1),
-    )
+        coupling,
+    )
+    integral_held, spread = lax.optimization_barrier((integral_last, spread))
+    base, extra = call(
+        base_kernel,
+        (local_shape, jax.ShapeDtypeStruct((hist_size, 16, wide), jnp.bfloat16)),
+        (SCALARS, *(OUTSIDE,) * 4),
+        [terms, *by_time, square, square, pltpu.SemaphoreType.DMA((4,))],
+    )(
+        hist_at.astype(jnp.int32)[None],
+        g_last.transpose(1, 0, 2),
+        integral_held.transpose(1, 0, 2),
+        step_re,
+        step_im,
+    )
+
     def contract(pieces, *extra):
         rows = padded + sum(value.shape[1] for value in extra)
         return call(
@@ -330,13 +341,11 @@
         )(pieces, history, *extra)
 
     piece = lax.dynamic_index_in_dim(exchange(spread, PLANE), hist_at, 0, keepdims=False)
+    piece, base, extra = lax.optimization_barrier((piece, base, extra))
     for iteration in range(ITERS):
         copies = jnp.broadcast_to(piece[None], (rows_size, padded, wide))
-        extra = (base_chunk(),) if iteration == 0 else ()
-        sent = contract(exchange(copies, ROWS), *extra)
-        if iteration == 0:
-            integral_held, sent = lax.optimization_barrier((integral_last, sent))
-            base = base_rows(integral_held)
+        pieces = exchange(copies, ROWS)
+        sent = contract(pieces, extra) if iteration == 0 else contract(pieces)
         if iteration < ITERS - 1:
             sent = exchange(sent, PLANE)
         arrived = exchange(sent, "hist")

time: 172 us -> 168 us (0.977)
  blocking collectives: 91.7 us -> 140 us
  waiting for transfers between devices: 40 us -> 5.42 us
  starting transfers between devices: 19.9 us -> 7.05 us
  local copies, waits for them, and re-layouts: 10.1 us -> 3.14 us
  Pallas kernels: 6.31 us -> 9.54 us
    all_to_all x5 -> x8, blocking collectives: 91.7 us -> 140 us  [exchange(): return lax.all_to_all(blocks, axes, split_axis=0, concat_axis=0, tiled=True)]
    all_to_all x4 -> x1, waiting for transfers between devices: 40 us -> 5.42 us  [exchange(): return lax.all_to_all(blocks, axes, split_axis=0, concat_axis=0, tiled=True)]
    all_to_all x4 -> x1, starting transfers between devices: 19.9 us -> 7.05 us  [exchange(): return lax.all_to_all(blocks, axes, split_axis=0, concat_axis=0, tiled=True)]
    dynamic_slice x4 -> x0, local copies, waits for them, and re-layouts: 3.11 us -> none  [the longest x2 1.6 us: some_times(): lax.dynamic_slice_in_dim(value, jnp.minimum(start + t, row_count - 1), 1, 0)]
    pallas_call x0 -> x1, Pallas kernels: none -> 2.72 us  [on_device(): call(base_kernel, (local_shape, jax.ShapeDtypeStruct((hist_size, 16, wide...]
    unnamed x12, local copies, waits for them, and re-layouts: 5.25 us -> 2.98 us
  transfers between devices with their start and end apart: 4 -> 1, of which waited for: 4 -> 1; matrix products, arithmetic and copies ran while one was open for 3% -> 0% of each run, Pallas kernels for 0% -> 2%
where the time goes in v5:
time: 168 us; the launch traced here: 167 us
  blocking collectives  140 us (83%)
  Pallas kernels  9.54 us (6%)
  starting transfers between devices  7.05 us (4%)
  waiting for transfers between devices  5.42 us (3%)
  local copies, waits for them, and re-layouts  3.14 us (2%)
    all_to_all x8, blocking collectives, exchange(): return lax.all_to_all(blocks, axes, split_axis=0, concat_axis=0, tiled=True)  140 us
    all_to_all x1, starting transfers between devices, exchange(): return lax.all_to_all(blocks, axes, split_axis=0, concat_axis=0, tiled=True)  7.05 us
    all_to_all x1, waiting for transfers between devices, exchange(): return lax.all_to_all(blocks, axes, split_axis=0, concat_axis=0, tiled=True)  5.42 us
  transfers between devices with their start and end apart: 1, of which 1 were waited for; matrix products, arithmetic and copies ran while one was open for 0% of the time, Pallas kernels for 2%

profile of v5, /device:TPU:32, one launch (start us, length us, event | category | flops | bytes accessed | tf_op | source)
XLA Modules:
  0.0 167.0 jit_solution(17525168446501709308)
XLA Ops:
  0.6 0.6 pad_add_fusion.at_ref
  1.2 2.7 %shard_map.77 = (bf16[16,48,128]{2,1,0:T(8,128)(2,1)}, f32[48,128]{1,0:T(8,128)}, f32[48,128]{1,0:T(8,128)}) custom-call(s32[3]{0:T(128)} %pad_add_fusion.at_ref, f32[11,64,128]{2,1,0:T(8,128)} %bitcast.14, f32[64,64]{1,0:T(8,128)} %refs_1_.1), custom_call_target="tpu_custom_call" | custom-call | tf_op jit(solution)/shard_map/pallas_call | solution.py:306
  3.9 7.0 %all-to-all-start = ((bf16[16,48,128]{2,1,0:T(8,128)(2,1)}), bf16[16,48,128]{2,1,0:T(8,128)(2,1)S(1)}, u32[]{:S(2)}, u32[]{:S(2)}) async-start(bf16[16,48,128]{2,1,0:T(8,128)(2,1)} %get-tuple-element.19), calls=%async_computation | async-start | bytes 393216 | tf_op jit(solution)/shard_map/all_to_all | solution.py:295
  11.0 0.0 copy-start.2
  11.0 0.0 copy-start.3
  11.0 2.7 %shard_map.78 = (f32[48,128]{1,0:T(8,128)}, bf16[16,16,128]{2,1,0:T(8,128)(2,1)}) custom-call(s32[1]{0:T(128)} %bitcast.5.at_ref, f32[11,64,128]{2,1,0:T(8,128)} %bitcast.15, f32[11,64,128]{2,1,0:T(8,128)} %bitcast.16, f32[64,64]{1,0:T(8,128)} %refs_2_.1, f32[64,64]{1,0:T(8,128)} %refs_3_.1), custom_call_target="tpu_custom_call" | custom-call | tf_op jit(solution)/shard_map/pallas_call | solution.py:317
  13.7 5.4 %all-to-all-done = bf16[16,48,128]{2,1,0:T(8,128)(2,1)S(1)} async-done(((bf16[16,48,128]{2,1,0:T(8,128)(2,1)}), bf16[16,48,128]{2,1,0:T(8,128)(2,1)S(1)}, u32[]{:S(2)}, u32[]{:S(2)}) %all-to-all-start) | async-done | bytes 196640 | tf_op jit(solution)/shard_map/all_to_all | solution.py:295
  19.1 0.1 broadcast_in_dim.9
  19.2 13.7 %all_to_all.45.pieces_ref = bf16[32,48,128]{2,1,0:T(8,128)(2,1)S(1)} all-to-all(bf16[32,48,128]{2,1,0:T(8,128)(2,1)S(1)} %broadcast_in_dim.9), channel_id=1, replica_groups=mesh['hist'=16,'rows_0'=4,'rows_1'=4,'rows_2'=2] {'rows_0','rows_1','row..., dimensions={0} | all-to-all | bytes 786432 | tf_op jit(solution)/shard_map/all_to_all | solution.py:295
  32.9 0.0 copy-start
  32.9 2.1 %copy-done = bf16[22,64,11,128]{3,1,2,0:T(8,128)(2,1)S(1)} copy-done((bf16[22,64,11,128]{3,1,2,0:T(8,128)(2,1)S(1)}, bf16[22,64,11,128]{3,1,2,0:T(8,128)(2,1)}, u32[]{:S(2)}) %copy-start) | copy-done | bytes 3964952
  35.0 0.0 copy-start.4
  35.0 0.8 copy-done.4
  35.8 0.0 copy-start.1
  35.8 0.9 shard_map.79
  36.8 12.5 %all_to_all.46 = bf16[16,64,128]{2,1,0:T(8,128)(2,1)S(1)} all-to-all(bf16[16,64,128]{2,1,0:T(8,128)(2,1)S(1)} %shard_map.79), channel_id=1, replica_groups=mesh['hist'=16,'rows_0'=4,'rows_1'=4,'rows_2'=2] {'rows_0','rows_1'}, dimensions={0} | all-to-all | bytes 524288 | tf_op jit(solution)/shard_map/all_to_all | solution.py:295
  49.2 32.7 %all_to_all.47.arrived_ref = bf16[16,64,128]{2,1,0:T(8,128)(2,1)S(1)} all-to-all(bf16[16,64,128]{2,1,0:T(8,128)(2,1)S(1)} %all_to_all.46), channel_id=1, replica_groups=mesh['hist'=16,'rows_0'=4,'rows_1'=4,'rows_2'=2] {'hist'}, dimensions={0} | all-to-all | bytes 524288 | tf_op jit(solution)/shard_map/all_to_all | solution.py:295
  82.0 0.0 copy-done.2
  82.0 0.0 copy-done.3
  82.0 0.3 shard_map.80
  82.3 0.1 broadcast_in_dim.10
  82.3 13.5 %all_to_all.48.pieces_ref = bf16[32,48,128]{2,1,0:T(8,128)(2,1)S(1)} all-to-all(bf16[32,48,128]{2,1,0:T(8,128)(2,1)S(1)} %broadcast_in_dim.10), channel_id=1, replica_groups=mesh['hist'=16,'rows_0'=4,'rows_1'=4,'rows_2'=2] {'rows_0','rows_1','row..., dimensions={0} | all-to-all | bytes 786432 | tf_op jit(solution)/shard_map/all_to_all | solution.py:295
  95.9 0.0 copy-done.1
  95.9 0.9 shard_map.81
  96.8 0.0 copy-start.5
  96.8 11.7 %all_to_all.49 = bf16[16,48,128]{2,1,0:T(8,128)(2,1)S(1)} all-to-all(bf16[16,48,128]{2,1,0:T(8,128)(2,1)S(1)} %shard_map.81), channel_id=1, replica_groups=mesh['hist'=16,'rows_0'=4,'rows_1'=4,'rows_2'=2] {'rows_0','rows_1'}, dimensions={0} | all-to-all | bytes 393216 | tf_op jit(solution)/shard_map/all_to_all | solution.py:295
  108.5 21.1 %all_to_all.50.arrived_ref = bf16[16,48,128]{2,1,0:T(8,128)(2,1)S(1)} all-to-all(bf16[16,48,128]{2,1,0:T(8,128)(2,1)S(1)} %all_to_all.49), channel_id=1, replica_groups=mesh['hist'=16,'rows_0'=4,'rows_1'=4,'rows_2'=2] {'hist'}, dimensions={0} | all-to-all | bytes 393216 | tf_op jit(solution)/shard_map/all_to_all | solution.py:295
  129.7 0.3 shard_map.82
  130.0 0.1 broadcast_in_dim.11
  130.0 14.2 %all_to_all.51.pieces_ref = bf16[32,48,128]{2,1,0:T(8,128)(2,1)S(1)} all-to-all(bf16[32,48,128]{2,1,0:T(8,128)(2,1)S(1)} %broadcast_in_dim.11), channel_id=1, replica_groups=mesh['hist'=16,'rows_0'=4,'rows_1'=4,'rows_2'=2] {'rows_0','rows_1','row..., dimensions={0} | all-to-all | bytes 786432 | tf_op jit(solution)/shard_map/all_to_all | solution.py:295
  144.2 1.0 shard_map.83
  145.2 21.1 %all_to_all.52.arrived_ref = bf16[16,48,128]{2,1,0:T(8,128)(2,1)S(1)} all-to-all(bf16[16,48,128]{2,1,0:T(8,128)(2,1)S(1)} %shard_map.83), channel_id=1, replica_groups=mesh['hist'=16,'rows_0'=4,'rows_1'=4,'rows_2'=2] {'hist'}, dimensions={0} | all-to-all | bytes 393216 | tf_op jit(solution)/shard_map/all_to_all | solution.py:295
  166.3 0.0 copy-done.5
  166.3 0.7 shard_map.84
  (1 shorter events, 0.0 us)
Async XLA Ops:
  3.9 15.2 %all-to-all-start = ((bf16[16,48,128]{2,1,0:T(8,128)(2,1)}), bf16[16,48,128]{2,1,0:T(8,128)(2,1)S(1)}, u32[]{:S(2)}, u32[]{:S(2)}) async-start(bf16[16,48,128]{2,1,0:T(8,128)(2,1)} %get-tuple-element.19), calls=%async_computation | async-start | bytes 393216 | tf_op jit(solution)/shard_map/all_to_all | solution.py:295
  11.0 71.0 %copy-start.2 = (f32[48,128]{1,0:T(8,128)S(1)}, f32[48,128]{1,0:T(8,128)}, u32[]{:S(2)}) copy-start(f32[48,128]{1,0:T(8,128)} %get-tuple-element.25.factor_ref) | copy-start | bytes 73732
  11.0 71.0 %copy-start.3 = (f32[48,128]{1,0:T(8,128)S(1)}, f32[48,128]{1,0:T(8,128)}, u32[]{:S(2)}) copy-start(f32[48,128]{1,0:T(8,128)} %get-tuple-element.26.mask_ref) | copy-start | bytes 73732
  32.9 2.1 %copy-start = (bf16[22,64,11,128]{3,1,2,0:T(8,128)(2,1)S(1)}, bf16[22,64,11,128]{3,1,2,0:T(8,128)(2,1)}, u32[]{:S(2)}) copy-start(bf16[22,64,11,128]{3,1,2,0:T(8,128)(2,1)} %param.6) | copy-start | bytes 11894788
  35.0 0.8 copy-start.4
  35.8 60.0 %copy-start.1 = (bf16[22,64,11,128]{3,1,2,0:T(8,128)(2,1)S(1)}, bf16[22,64,11,128]{3,1,2,0:T(8,128)(2,1)}, u32[]{:S(2)}) copy-start(bf16[22,64,11,128]{3,1,2,0:T(8,128)(2,1)} %param.6) | copy-start | bytes 11894788
  96.8 69.5 %copy-start.5 = (f32[48,128]{1,0:T(8,128)S(1)}, f32[48,128]{1,0:T(8,128)}, u32[]{:S(2)}) copy-start(f32[48,128]{1,0:T(8,128)} %get-tuple-element.30.base_ref) | copy-start | bytes 73732

commit v6 on v5

--- a/solution.py
+++ b/solution.py
@@ -20,7 +20,6 @@
 half_step = 0.25
 
 
-SCALARS = pl.BlockSpec(memory_space=pltpu.SMEM)
 VECTORS = pl.BlockSpec(memory_space=pltpu.VMEM)
 OUTSIDE = pl.BlockSpec(memory_space=pltpu.HBM)
 
@@ -33,8 +32,12 @@
         in_specs=specs,
         out_specs=outs,
         scratch_shapes=list(scratch),
-        compiler_params=pltpu.CompilerParams(vmem_limit_bytes=None if OUTSIDE in specs else SMALL_VMEM),
-    )
+        compiler_params=pltpu.CompilerParams(vmem_limit_bytes=SMALL_VMEM),
+    )
+
+
+def far(value):
+    return pltpu.with_memory_space_constraint(value, pltpu.HBM)
 
 
 def low_half(shape):
@@ -86,11 +89,13 @@
     )
 
 
-def first_kernel(at_ref, *refs, share):
+def first_kernel(*refs, share):
     pieces_ref, factor_ref, mask_ref, terms_ref = refs[2:6]
     rows_ref, coupling_ref = refs[6:8]
     fetch(refs[:2], refs[6:8], refs[8])
-    rows_at, plane_at, block_at = at_ref[0], at_ref[1], at_ref[2]
+    rows_at = lax.axis_index(ROWS)
+    plane_at = lax.axis_index(PLANE)
+    block_at = lax.axis_index("hist") * lax.axis_size(ROWS[-1]) + lax.axis_index(ROWS[-1])
     times, orbits, wide = rows_ref.shape
     count, padded, _ = pieces_ref.shape
     row = lax.broadcasted_iota(jnp.int32, (orbits, wide), 0)
@@ -134,11 +139,11 @@
         mask_ref[8 * group : 8 * group + 8, :] = kept
 
 
-def base_kernel(at_ref, *refs):
+def base_kernel(*refs):
     base_ref, extra_ref, terms_ref = refs[4:7]
     rows_ref, integrals_ref, step_re_ref, step_im_ref = refs[7:11]
     fetch(refs[:4], refs[7:11], refs[11])
-    hist_at = at_ref[0]
+    hist_at = lax.axis_index("hist")
     times, orbits, wide = rows_ref.shape
     count = extra_ref.shape[0]
     padded = base_ref.shape[0]
@@ -284,9 +289,6 @@
     rows_size = lax.axis_size(ROWS)
     fan_out = rows_size // hist_size
     hist_at = lax.axis_index("hist")
-    rows_at = lax.axis_index(ROWS)
-    plane_at = lax.axis_index(PLANE)
-    core_at = lax.axis_index(ROWS[-1])
     total_cells = row_count * rows_size * orbits
     share = orbits // hist_size
     cells = share * row_count
@@ -306,46 +308,44 @@
     spread, factor, mask = call(
         functools.partial(first_kernel, share=share),
         (pieces_shape, local_shape, local_shape),
-        (SCALARS, OUTSIDE, OUTSIDE),
+        (OUTSIDE,) * 2,
         [terms, *by_time[:1], square, pltpu.SemaphoreType.DMA((2,))],
     )(
-        jnp.stack([rows_at, plane_at, hist_at * fan_out + core_at]).astype(jnp.int32),
-        g_last.transpose(1, 0, 2),
-        coupling,
+        far(g_last.transpose(1, 0, 2)),
+        far(coupling),
     )
     integral_held, spread = lax.optimization_barrier((integral_last, spread))
     base, extra = call(
         base_kernel,
-        (local_shape, jax.ShapeDtypeStruct((hist_size, 16, wide), jnp.bfloat16)),
-        (SCALARS, *(OUTSIDE,) * 4),
+        (local_shape, jax.ShapeDtypeStruct((hist_size, 8, wide), jnp.bfloat16)),
+        (OUTSIDE,) * 4,
         [terms, *by_time, square, square, pltpu.SemaphoreType.DMA((4,))],
     )(
-        hist_at.astype(jnp.int32)[None],
-        g_last.transpose(1, 0, 2),
-        integral_held.transpose(1, 0, 2),
-        step_re,
-        step_im,
-    )
-
-    def contract(pieces, *extra):
-        rows = padded + sum(value.shape[1] for value in extra)
+        far(g_last.transpose(1, 0, 2)),
+        far(integral_held.transpose(1, 0, 2)),
+        far(step_re),
+        far(step_im),
+    )
+
+    def contract(*operands):
+        rows = padded + sum(value.shape[1] for value in operands[2:])
         return call(
             functools.partial(contract_kernel, times=row_count),
             jax.ShapeDtypeStruct((hist_size, rows, wide), jnp.bfloat16),
-            (VECTORS,) * (2 + len(extra)),
+            (VECTORS,) * len(operands),
             [
                 pltpu.VMEM((fan_out, 2, padded // 8, orbits, wide), jnp.float32),
                 pltpu.VMEM((wide, fan_out * row_count * orbits), jnp.bfloat16),
                 terms,
             ],
-        )(pieces, history, *extra)
+        )(*operands)
 
     piece = lax.dynamic_index_in_dim(exchange(spread, PLANE), hist_at, 0, keepdims=False)
     piece, base, extra = lax.optimization_barrier((piece, base, extra))
     for iteration in range(ITERS):
         copies = jnp.broadcast_to(piece[None], (rows_size, padded, wide))
         pieces = exchange(copies, ROWS)
-        sent = contract(pieces, extra) if iteration == 0 else contract(pieces)
+        sent = contract(pieces, history, *([extra] if iteration == 0 else []))
         if iteration < ITERS - 1:
             sent = exchange(sent, PLANE)
         arrived = exchange(sent, "hist")

time: 168 us -> 164 us (0.976)
    all_to_all x8, blocking collectives: 140 us -> 139 us  [exchange(): return lax.all_to_all(blocks, axes, split_axis=0, concat_axis=0, tiled=True)]
  transfers between devices with their start and end apart: 1 -> 1, of which waited for: 1 -> 1; matrix products, arithmetic and copies ran while one was open for 0% -> 0% of each run, Pallas kernels for 2% -> 1%
where the time goes in v6:
time: 164 us; the launch traced here: 163 us
  blocking collectives  139 us (85%)
  Pallas kernels  8.21 us (5%)
  starting transfers between devices  7.05 us (4%)
  waiting for transfers between devices  6.07 us (4%)
  local copies, waits for them, and re-layouts  2.29 us (1%)
    all_to_all x8, blocking collectives, exchange(): return lax.all_to_all(blocks, axes, split_axis=0, concat_axis=0, tiled=True)  139 us
    all_to_all x1, starting transfers between devices, exchange(): return lax.all_to_all(blocks, axes, split_axis=0, concat_axis=0, tiled=True)  7.05 us
    all_to_all x1, waiting for transfers between devices, exchange(): return lax.all_to_all(blocks, axes, split_axis=0, concat_axis=0, tiled=True)  6.07 us
  transfers between devices with their start and end apart: 1, of which 1 were waited for; matrix products, arithmetic and copies ran while one was open for 0% of the time, Pallas kernels for 1%

profile of v6, /device:TPU:32, one launch (start us, length us, event | category | flops | bytes accessed | tf_op | source)
XLA Modules:
  0.0 163.0 jit_solution(15619776535403465468)
XLA Ops:
  0.6 2.0 %shard_map.77 = (bf16[16,48,128]{2,1,0:T(8,128)(2,1)}, f32[48,128]{1,0:T(8,128)S(1)}, f32[48,128]{1,0:T(8,128)S(1)}) custom-call(f32[11,64,128]{2,1,0:T(8,128)} %bitcast.10, f32[64,64]{1,0:T(8,128)} %refs_1_.1), custom_call_target="tpu_custom_call" | custom-call | tf_op jit(solution)/shard_map/pallas_call | solution.py:308
  2.6 7.0 %all-to-all-start = ((bf16[16,48,128]{2,1,0:T(8,128)(2,1)}), bf16[16,48,128]{2,1,0:T(8,128)(2,1)S(1)}, u32[]{:S(2)}, u32[]{:S(2)}) async-start(bf16[16,48,128]{2,1,0:T(8,128)(2,1)} %get-tuple-element.19), calls=%async_computation | async-start | bytes 393216 | tf_op jit(solution)/shard_map/all_to_all | solution.py:297
  9.7 2.1 %shard_map.78 = (f32[48,128]{1,0:T(8,128)S(1)}, bf16[16,8,128]{2,1,0:T(8,128)(2,1)S(1)}) custom-call(f32[11,64,128]{2,1,0:T(8,128)} %bitcast.11, f32[11,64,128]{2,1,0:T(8,128)} %bitcast.12, f32[64,64]{1,0:T(8,128)} %refs_2_.1, f32[64,64]{1,0:T(8,128)} %refs_3_.1), custom_call_target="tpu_custom_call" | custom-call | tf_op jit(solution)/shard_map/pallas_call | solution.py:318
  11.8 6.1 %all-to-all-done = bf16[16,48,128]{2,1,0:T(8,128)(2,1)S(1)} async-done(((bf16[16,48,128]{2,1,0:T(8,128)(2,1)}), bf16[16,48,128]{2,1,0:T(8,128)(2,1)S(1)}, u32[]{:S(2)}, u32[]{:S(2)}) %all-to-all-start) | async-done | bytes 196640 | tf_op jit(solution)/shard_map/all_to_all | solution.py:297
  17.9 0.1 broadcast_in_dim.6
  17.9 13.7 %all_to_all.45.pieces_ref = bf16[32,48,128]{2,1,0:T(8,128)(2,1)S(1)} all-to-all(bf16[32,48,128]{2,1,0:T(8,128)(2,1)S(1)} %broadcast_in_dim.6), channel_id=1, replica_groups=mesh['hist'=16,'rows_0'=4,'rows_1'=4,'rows_2'=2] {'rows_0','rows_1','row..., dimensions={0} | all-to-all | bytes 786432 | tf_op jit(solution)/shard_map/all_to_all | solution.py:297
  31.6 0.0 copy-start
  31.6 2.1 %copy-done = bf16[22,64,11,128]{3,1,2,0:T(8,128)(2,1)S(1)} copy-done((bf16[22,64,11,128]{3,1,2,0:T(8,128)(2,1)S(1)}, bf16[22,64,11,128]{3,1,2,0:T(8,128)(2,1)}, u32[]{:S(2)}) %copy-start) | copy-done | bytes 3964952
  33.7 0.0 copy-start.1
  33.7 0.9 shard_map.79
  34.6 12.1 %all_to_all.46 = bf16[16,56,128]{2,1,0:T(8,128)(2,1)S(1)} all-to-all(bf16[16,56,128]{2,1,0:T(8,128)(2,1)S(1)} %shard_map.79), channel_id=1, replica_groups=mesh['hist'=16,'rows_0'=4,'rows_1'=4,'rows_2'=2] {'rows_0','rows_1'}, dimensions={0} | all-to-all | bytes 458752 | tf_op jit(solution)/shard_map/all_to_all | solution.py:297
  46.8 31.7 %all_to_all.47.arrived_ref = bf16[16,56,128]{2,1,0:T(8,128)(2,1)S(1)} all-to-all(bf16[16,56,128]{2,1,0:T(8,128)(2,1)S(1)} %all_to_all.46), channel_id=1, replica_groups=mesh['hist'=16,'rows_0'=4,'rows_1'=4,'rows_2'=2] {'hist'}, dimensions={0} | all-to-all | bytes 458752 | tf_op jit(solution)/shard_map/all_to_all | solution.py:297
  78.4 0.3 shard_map.80
  78.8 0.1 broadcast_in_dim.7
  78.8 13.8 %all_to_all.48.pieces_ref = bf16[32,48,128]{2,1,0:T(8,128)(2,1)S(1)} all-to-all(bf16[32,48,128]{2,1,0:T(8,128)(2,1)S(1)} %broadcast_in_dim.7), channel_id=1, replica_groups=mesh['hist'=16,'rows_0'=4,'rows_1'=4,'rows_2'=2] {'rows_0','rows_1','row..., dimensions={0} | all-to-all | bytes 786432 | tf_op jit(solution)/shard_map/all_to_all | solution.py:297
  92.6 0.0 copy-done.1
  92.6 0.9 shard_map.81
  93.6 11.7 %all_to_all.49 = bf16[16,48,128]{2,1,0:T(8,128)(2,1)S(1)} all-to-all(bf16[16,48,128]{2,1,0:T(8,128)(2,1)S(1)} %shard_map.81), channel_id=1, replica_groups=mesh['hist'=16,'rows_0'=4,'rows_1'=4,'rows_2'=2] {'rows_0','rows_1'}, dimensions={0} | all-to-all | bytes 393216 | tf_op jit(solution)/shard_map/all_to_all | solution.py:297
  105.3 20.5 %all_to_all.50.arrived_ref = bf16[16,48,128]{2,1,0:T(8,128)(2,1)S(1)} all-to-all(bf16[16,48,128]{2,1,0:T(8,128)(2,1)S(1)} %all_to_all.49), channel_id=1, replica_groups=mesh['hist'=16,'rows_0'=4,'rows_1'=4,'rows_2'=2] {'hist'}, dimensions={0} | all-to-all | bytes 393216 | tf_op jit(solution)/shard_map/all_to_all | solution.py:297
  125.7 0.3 shard_map.82
  126.1 0.1 broadcast_in_dim.8
  126.1 14.2 %all_to_all.51.pieces_ref = bf16[32,48,128]{2,1,0:T(8,128)(2,1)S(1)} all-to-all(bf16[32,48,128]{2,1,0:T(8,128)(2,1)S(1)} %broadcast_in_dim.8), channel_id=1, replica_groups=mesh['hist'=16,'rows_0'=4,'rows_1'=4,'rows_2'=2] {'rows_0','rows_1','row..., dimensions={0} | all-to-all | bytes 786432 | tf_op jit(solution)/shard_map/all_to_all | solution.py:297
  140.3 0.9 shard_map.83
  141.2 21.1 %all_to_all.52.arrived_ref = bf16[16,48,128]{2,1,0:T(8,128)(2,1)S(1)} all-to-all(bf16[16,48,128]{2,1,0:T(8,128)(2,1)S(1)} %shard_map.83), channel_id=1, replica_groups=mesh['hist'=16,'rows_0'=4,'rows_1'=4,'rows_2'=2] {'hist'}, dimensions={0} | all-to-all | bytes 393216 | tf_op jit(solution)/shard_map/all_to_all | solution.py:297
  162.3 0.7 shard_map.84
  (1 shorter events, 0.0 us)
Async XLA Ops:
  2.6 15.2 %all-to-all-start = ((bf16[16,48,128]{2,1,0:T(8,128)(2,1)}), bf16[16,48,128]{2,1,0:T(8,128)(2,1)S(1)}, u32[]{:S(2)}, u32[]{:S(2)}) async-start(bf16[16,48,128]{2,1,0:T(8,128)(2,1)} %get-tuple-element.19), calls=%async_computation | async-start | bytes 393216 | tf_op jit(solution)/shard_map/all_to_all | solution.py:297
  31.6 2.1 %copy-start = (bf16[22,64,11,128]{3,1,2,0:T(8,128)(2,1)S(1)}, bf16[22,64,11,128]{3,1,2,0:T(8,128)(2,1)}, u32[]{:S(2)}) copy-start(bf16[22,64,11,128]{3,1,2,0:T(8,128)(2,1)} %param.6) | copy-start | bytes 11894788
  33.7 58.9 %copy-start.1 = (bf16[22,64,11,128]{3,1,2,0:T(8,128)(2,1)S(1)}, bf16[22,64,11,128]{3,1,2,0:T(8,128)(2,1)}, u32[]{:S(2)}) copy-start(bf16[22,64,11,128]{3,1,2,0:T(8,128)(2,1)} %param.6) | copy-start | bytes 11894788

commit v7 on v6

--- a/solution.py
+++ b/solution.py
@@ -24,7 +24,7 @@
 OUTSIDE = pl.BlockSpec(memory_space=pltpu.HBM)
 
 
-def call(kernel, shape, specs, scratch=()):
+def call(kernel, shape, specs, scratch=(), cost=None):
     outs = (VECTORS,) * len(shape) if isinstance(shape, tuple) else VECTORS
     return pl.pallas_call(
         kernel,
@@ -32,6 +32,7 @@
         in_specs=specs,
         out_specs=outs,
         scratch_shapes=list(scratch),
+        cost_estimate=cost,
         compiler_params=pltpu.CompilerParams(vmem_limit_bytes=SMALL_VMEM),
     )
 
@@ -178,6 +179,12 @@
             extra = jnp.where(row == at, high, extra)
             extra = jnp.where(row == parts + at, value - high, extra)
         extra_ref[share] = extra.astype(extra_ref.dtype)
+
+
+def spread_kernel(blocks_ref, copies_ref):
+    block = blocks_ref[lax.axis_index("hist")]
+    for at in range(copies_ref.shape[0]):
+        copies_ref[at] = block
 
 
 def advance(arrived_ref, base_ref, restore, cells, total_cells):
@@ -288,7 +295,6 @@
     hist_size = lax.axis_size("hist")
     rows_size = lax.axis_size(ROWS)
     fan_out = rows_size // hist_size
-    hist_at = lax.axis_index("hist")
     total_cells = row_count * rows_size * orbits
     share = orbits // hist_size
     cells = share * row_count
@@ -340,10 +346,12 @@
             ],
         )(*operands)
 
-    piece = lax.dynamic_index_in_dim(exchange(spread, PLANE), hist_at, 0, keepdims=False)
-    piece, base, extra = lax.optimization_barrier((piece, base, extra))
+    copies_shape = jax.ShapeDtypeStruct((rows_size, padded, wide), jnp.bfloat16)
+    copies = call(spread_kernel, copies_shape, (VECTORS,), (), pl.CostEstimate(flops=2000000000, bytes_accessed=400000, transcendentals=0))(exchange(spread, PLANE))
+    copies, base, extra = lax.optimization_barrier((copies, base, extra))
     for iteration in range(ITERS):
-        copies = jnp.broadcast_to(piece[None], (rows_size, padded, wide))
+        if iteration > 0:
+            copies = jnp.broadcast_to(piece[None], copies_shape.shape)
         pieces = exchange(copies, ROWS)
         sent = contract(pieces, history, *([extra] if iteration == 0 else []))
         if iteration < ITERS - 1:

time: 164 us -> 162 us (0.988)
  local copies, waits for them, and re-layouts: 2.29 us -> 0.11 us
    unnamed x4 -> x2, local copies, waits for them, and re-layouts: 2.13 us -> 0.01 us
where the time goes in v7:
time: 162 us; the launch traced here: 161 us
  blocking collectives  139 us (86%)
  Pallas kernels  8.25 us (5%)
  starting transfers between devices  7.05 us (4%)
  waiting for transfers between devices  6.08 us (4%)
    all_to_all x8, blocking collectives, exchange(): return lax.all_to_all(blocks, axes, split_axis=0, concat_axis=0, tiled=True)  139 us
    all_to_all x1, starting transfers between devices, exchange(): return lax.all_to_all(blocks, axes, split_axis=0, concat_axis=0, tiled=True)  7.05 us
    all_to_all x1, waiting for transfers between devices, exchange(): return lax.all_to_all(blocks, axes, split_axis=0, concat_axis=0, tiled=True)  6.08 us
  transfers between devices with their start and end apart: 1, of which 1 were waited for; matrix products, arithmetic and copies ran while one was open for 0% of the time, Pallas kernels for 1%

profile of v7, /device:TPU:32, one launch (start us, length us, event | category | flops | bytes accessed | tf_op | source)
XLA Modules:
  0.0 161.0 jit_solution(8812076704665745635)
XLA Ops:
  0.6 2.0 %shard_map.77 = (bf16[16,48,128]{2,1,0:T(8,128)(2,1)}, f32[48,128]{1,0:T(8,128)S(1)}, f32[48,128]{1,0:T(8,128)S(1)}) custom-call(f32[11,64,128]{2,1,0:T(8,128)} %bitcast.8, f32[64,64]{1,0:T(8,128)} %refs_1_.1), custom_call_target="tpu_custom_call" | custom-call | tf_op jit(solution)/shard_map/pallas_call | solution.py:314
  2.6 7.0 %all-to-all-start = ((bf16[16,48,128]{2,1,0:T(8,128)(2,1)}), bf16[16,48,128]{2,1,0:T(8,128)(2,1)S(1)}, u32[]{:S(2)}, u32[]{:S(2)}) async-start(bf16[16,48,128]{2,1,0:T(8,128)(2,1)} %get-tuple-element.19), calls=%async_computation | async-start | bytes 393216 | tf_op jit(solution)/shard_map/all_to_all | solution.py:303
  9.7 2.1 %shard_map.79 = (f32[48,128]{1,0:T(8,128)S(1)}, bf16[16,8,128]{2,1,0:T(8,128)(2,1)S(1)}) custom-call(f32[11,64,128]{2,1,0:T(8,128)} %bitcast.9, f32[11,64,128]{2,1,0:T(8,128)} %bitcast.10, f32[64,64]{1,0:T(8,128)} %refs_2_.1, f32[64,64]{1,0:T(8,128)} %refs_3_.1), custom_call_target="tpu_custom_call" | custom-call | tf_op jit(solution)/shard_map/pallas_call | solution.py:324
  11.8 6.1 %all-to-all-done.blocks_ref = bf16[16,48,128]{2,1,0:T(8,128)(2,1)S(1)} async-done(((bf16[16,48,128]{2,1,0:T(8,128)(2,1)}), bf16[16,48,128]{2,1,0:T(8,128)(2,1)S(1)}, u32[]{:S(2)}, u32[]{:S(2)}) %all-to-all-start) | async-done | bytes 196640 | tf_op jit(solution)/shard_map/all_to_all | solution.py:303
  17.9 0.0 copy-start
  17.9 0.1 shard_map.78
  17.9 13.9 %all_to_all.45.pieces_ref = bf16[32,48,128]{2,1,0:T(8,128)(2,1)S(1)} all-to-all(bf16[32,48,128]{2,1,0:T(8,128)(2,1)S(1)} %shard_map.78), channel_id=1, replica_groups=mesh['hist'=16,'rows_0'=4,'rows_1'=4,'rows_2'=2] {'rows_0','rows_1','row..., dimensions={0} | all-to-all | bytes 786432 | tf_op jit(solution)/shard_map/all_to_all | solution.py:303
  31.8 0.0 copy-done
  31.8 0.9 shard_map.80
  32.8 12.0 %all_to_all.46 = bf16[16,56,128]{2,1,0:T(8,128)(2,1)S(1)} all-to-all(bf16[16,56,128]{2,1,0:T(8,128)(2,1)S(1)} %shard_map.80), channel_id=1, replica_groups=mesh['hist'=16,'rows_0'=4,'rows_1'=4,'rows_2'=2] {'rows_0','rows_1'}, dimensions={0} | all-to-all | bytes 458752 | tf_op jit(solution)/shard_map/all_to_all | solution.py:303
  44.8 31.7 %all_to_all.47.arrived_ref = bf16[16,56,128]{2,1,0:T(8,128)(2,1)S(1)} all-to-all(bf16[16,56,128]{2,1,0:T(8,128)(2,1)S(1)} %all_to_all.46), channel_id=1, replica_groups=mesh['hist'=16,'rows_0'=4,'rows_1'=4,'rows_2'=2] {'hist'}, dimensions={0} | all-to-all | bytes 458752 | tf_op jit(solution)/shard_map/all_to_all | solution.py:303
  76.5 0.3 shard_map.81
  76.8 0.1 broadcast_in_dim.4
  76.8 13.8 %all_to_all.48.pieces_ref = bf16[32,48,128]{2,1,0:T(8,128)(2,1)S(1)} all-to-all(bf16[32,48,128]{2,1,0:T(8,128)(2,1)S(1)} %broadcast_in_dim.4), channel_id=1, replica_groups=mesh['hist'=16,'rows_0'=4,'rows_1'=4,'rows_2'=2] {'rows_0','rows_1','row..., dimensions={0} | all-to-all | bytes 786432 | tf_op jit(solution)/shard_map/all_to_all | solution.py:303
  90.6 0.9 shard_map.82
  91.6 11.7 %all_to_all.49 = bf16[16,48,128]{2,1,0:T(8,128)(2,1)S(1)} all-to-all(bf16[16,48,128]{2,1,0:T(8,128)(2,1)S(1)} %shard_map.82), channel_id=1, replica_groups=mesh['hist'=16,'rows_0'=4,'rows_1'=4,'rows_2'=2] {'rows_0','rows_1'}, dimensions={0} | all-to-all | bytes 393216 | tf_op jit(solution)/shard_map/all_to_all | solution.py:303
  103.3 20.5 %all_to_all.50.arrived_ref = bf16[16,48,128]{2,1,0:T(8,128)(2,1)S(1)} all-to-all(bf16[16,48,128]{2,1,0:T(8,128)(2,1)S(1)} %all_to_all.49), channel_id=1, replica_groups=mesh['hist'=16,'rows_0'=4,'rows_1'=4,'rows_2'=2] {'hist'}, dimensions={0} | all-to-all | bytes 393216 | tf_op jit(solution)/shard_map/all_to_all | solution.py:303
  123.7 0.3 shard_map.83
  124.1 0.1 broadcast_in_dim.5
  124.1 14.2 %all_to_all.51.pieces_ref = bf16[32,48,128]{2,1,0:T(8,128)(2,1)S(1)} all-to-all(bf16[32,48,128]{2,1,0:T(8,128)(2,1)S(1)} %broadcast_in_dim.5), channel_id=1, replica_groups=mesh['hist'=16,'rows_0'=4,'rows_1'=4,'rows_2'=2] {'rows_0','rows_1','row..., dimensions={0} | all-to-all | bytes 786432 | tf_op jit(solution)/shard_map/all_to_all | solution.py:303
  138.3 0.9 shard_map.84
  139.2 21.1 %all_to_all.52.arrived_ref = bf16[16,48,128]{2,1,0:T(8,128)(2,1)S(1)} all-to-all(bf16[16,48,128]{2,1,0:T(8,128)(2,1)S(1)} %shard_map.84), channel_id=1, replica_groups=mesh['hist'=16,'rows_0'=4,'rows_1'=4,'rows_2'=2] {'hist'}, dimensions={0} | all-to-all | bytes 393216 | tf_op jit(solution)/shard_map/all_to_all | solution.py:303
  160.3 0.7 shard_map.85
Async XLA Ops:
  2.6 15.2 %all-to-all-start = ((bf16[16,48,128]{2,1,0:T(8,128)(2,1)}), bf16[16,48,128]{2,1,0:T(8,128)(2,1)S(1)}, u32[]{:S(2)}, u32[]{:S(2)}) async-start(bf16[16,48,128]{2,1,0:T(8,128)(2,1)} %get-tuple-element.19), calls=%async_computation | async-start | bytes 393216 | tf_op jit(solution)/shard_map/all_to_all | solution.py:303
  17.9 14.0 %copy-start = (bf16[22,64,11,128]{3,1,2,0:T(8,128)(2,1)S(1)}, bf16[22,64,11,128]{3,1,2,0:T(8,128)(2,1)}, u32[]{:S(2)}) copy-start(bf16[22,64,11,128]{3,1,2,0:T(8,128)(2,1)} %param.6) | copy-start | bytes 11894788

commit v8 on v7

--- a/solution.py
+++ b/solution.py
@@ -90,37 +90,38 @@
     )
 
 
-def first_kernel(*refs, share):
-    pieces_ref, factor_ref, mask_ref, terms_ref = refs[2:6]
-    rows_ref, coupling_ref = refs[6:8]
-    fetch(refs[:2], refs[6:8], refs[8])
-    rows_at = lax.axis_index(ROWS)
-    plane_at = lax.axis_index(PLANE)
-    block_at = lax.axis_index("hist") * lax.axis_size(ROWS[-1]) + lax.axis_index(ROWS[-1])
+def first_kernel(source_ref, coupling_source_ref, pieces_ref, terms_ref, rows_ref, coupling_ref, sems):
     times, orbits, wide = rows_ref.shape
     count, padded, _ = pieces_ref.shape
+    share = orbits // count
+    fetch((source_ref, coupling_source_ref), (rows_ref, coupling_ref), sems)
     row = lax.broadcasted_iota(jnp.int32, (orbits, wide), 0)
     lane = lax.broadcasted_iota(jnp.int32, (orbits, wide), 1)
     own = coupling_ref[...] * step_size
     own = jnp.concatenate([own, own], -1)
+    early = jnp.where(lax.axis_index(ROWS) == 0, own * 0.5, own)
     power = jnp.zeros((orbits, wide), jnp.float32)
     peak = jnp.zeros((orbits, wide), jnp.float32)
-    values = []
-    for t in range(times):
-        field = rows_ref[t]
-        square = field * field
-        square = square + swapped(square)
-        power = power + jnp.where(lane == row, square, 0.0)
-        peak = jnp.maximum(peak, square)
-        scaled = jnp.where(rows_at == 0, own * 0.5, own) if t == 0 else own
-        values.append(scaled * square * field)
-    power = jnp.sum(power, axis=(0, 1), keepdims=True)
-    peak = jnp.max(peak, axis=(0, 1), keepdims=True)
-    values.append(notes(row % share, 0, jnp.where(row < share, power, 0.0), peak))
     for pair in range(padded // 8):
-        terms_ref[:, 0, pair], terms_ref[:, 1, pair] = packed(*values[2 * pair : 2 * pair + 2])
+        values = []
+        for t in range(2 * pair, min(2 * pair + 2, times)):
+            field = rows_ref[t]
+            square = field * field
+            square = square + swapped(square)
+            power = power + jnp.where(lane == row, square, 0.0)
+            peak = jnp.maximum(peak, square)
+            values.append((early if t == 0 else own) * square * field)
+        if len(values) < 2:
+            power = jnp.sum(power, axis=(0, 1), keepdims=True)
+            peak = jnp.max(peak, axis=(0, 1), keepdims=True)
+            values.append(notes(row % share, 0, jnp.where(row < share, power, 0.0), peak))
+        terms_ref[:, 0, pair], terms_ref[:, 1, pair] = packed(*values)
     pieces_ref[...] = terms_ref[...].reshape(count, padded, wide).astype(pieces_ref.dtype)
 
+
+def write_later(factor_ref, mask_ref, coupling_ref, times, share):
+    plane_at = lax.axis_index(PLANE)
+    block_at = lax.axis_index("hist") * lax.axis_size(ROWS[-1]) + lax.axis_index(ROWS[-1])
     start = pl.multiple_of(plane_at // 2 * 8, 8)
     mine = coupling_ref[pl.ds(start, 8), :] * step_size
     mine = jnp.concatenate([mine, mine], -1)
@@ -130,7 +131,7 @@
     upper = row < share
     factor = jnp.where(upper == (plane_at % 2 == 0), mine, turned)
     mask = jnp.where(lane == plane_at * share + row % share, 1.0, 0.0)
-    for group in range(padded // 8):
+    for group in range(factor_ref.shape[0] // 8):
         scaled, kept = factor, mask
         if group == 0:
             scaled = jnp.where(upper & (block_at == 0), factor * 0.5, factor)
@@ -141,13 +142,14 @@
 
 
 def base_kernel(*refs):
-    base_ref, extra_ref, terms_ref = refs[4:7]
-    rows_ref, integrals_ref, step_re_ref, step_im_ref = refs[7:11]
-    fetch(refs[:4], refs[7:11], refs[11])
+    base_ref, extra_ref, factor_ref, mask_ref, terms_ref = refs[5:10]
+    rows_ref, integrals_ref, step_re_ref, step_im_ref, coupling_ref = held = refs[10:15]
+    fetch(refs[:5], held, refs[15])
     hist_at = lax.axis_index("hist")
     times, orbits, wide = rows_ref.shape
     count = extra_ref.shape[0]
     padded = base_ref.shape[0]
+    write_later(factor_ref, mask_ref, coupling_ref, times, orbits // count)
     low = low_half((orbits, wide))
     sign = jnp.where(low, half_step, -half_step)
     turn = jnp.where(low, -1.0, 1.0)
@@ -311,26 +313,29 @@
     terms = pltpu.VMEM((hist_size // 2, 2, padded // 8, 8, wide), jnp.float32)
     by_time = [pltpu.VMEM((row_count, orbits, wide), jnp.float32)] * 2
     square = pltpu.VMEM((orbits, orbits), jnp.float32)
-    spread, factor, mask = call(
-        functools.partial(first_kernel, share=share),
-        (pieces_shape, local_shape, local_shape),
+    spread = call(
+        first_kernel,
+        pieces_shape,
         (OUTSIDE,) * 2,
         [terms, *by_time[:1], square, pltpu.SemaphoreType.DMA((2,))],
-    )(
-        far(g_last.transpose(1, 0, 2)),
-        far(coupling),
-    )
+    )(far(g_last.transpose(1, 0, 2)), far(coupling))
     integral_held, spread = lax.optimization_barrier((integral_last, spread))
-    base, extra = call(
+    base, extra, factor, mask = call(
         base_kernel,
-        (local_shape, jax.ShapeDtypeStruct((hist_size, 8, wide), jnp.bfloat16)),
-        (OUTSIDE,) * 4,
-        [terms, *by_time, square, square, pltpu.SemaphoreType.DMA((4,))],
+        (
+            local_shape,
+            jax.ShapeDtypeStruct((hist_size, 8, wide), jnp.bfloat16),
+            local_shape,
+            local_shape,
+        ),
+        (OUTSIDE,) * 5,
+        [terms, *by_time, *[square] * 3, pltpu.SemaphoreType.DMA((5,))],
     )(
         far(g_last.transpose(1, 0, 2)),
         far(integral_held.transpose(1, 0, 2)),
         far(step_re),
         far(step_im),
+        far(coupling),
     )
 
     def contract(*operands):

time: 162 us -> 162 us (level)
  no operation moved by 1% of the time
where the time goes in v8:
time: 162 us; the launch traced here: 161 us
  blocking collectives  139 us (86%)
  Pallas kernels  8.27 us (5%)
  starting transfers between devices  7.05 us (4%)
  waiting for transfers between devices  6.06 us (4%)
    all_to_all x8, blocking collectives, exchange(): return lax.all_to_all(blocks, axes, split_axis=0, concat_axis=0, tiled=True)  139 us
    all_to_all x1, starting transfers between devices, exchange(): return lax.all_to_all(blocks, axes, split_axis=0, concat_axis=0, tiled=True)  7.05 us
    all_to_all x1, waiting for transfers between devices, exchange(): return lax.all_to_all(blocks, axes, split_axis=0, concat_axis=0, tiled=True)  6.06 us
  transfers between devices with their start and end apart: 1, of which 1 were waited for; matrix products, arithmetic and copies ran while one was open for 0% of the time, Pallas kernels for 1%

profile of v8, /device:TPU:32, one launch (start us, length us, event | category | flops | bytes accessed | tf_op | source)
XLA Modules:
  0.0 161.1 jit_solution(10819769434782074113)
XLA Ops:
  0.6 2.0 %shard_map.77 = bf16[16,48,128]{2,1,0:T(8,128)(2,1)} custom-call(f32[11,64,128]{2,1,0:T(8,128)} %bitcast.8, f32[64,64]{1,0:T(8,128)} %refs_4_.1), custom_call_target="tpu_custom_call" | custom-call | tf_op jit(solution)/shard_map/pallas_call | solution.py:316
  2.6 7.0 %all-to-all-start = ((bf16[16,48,128]{2,1,0:T(8,128)(2,1)}), bf16[16,48,128]{2,1,0:T(8,128)(2,1)S(1)}, u32[]{:S(2)}, u32[]{:S(2)}) async-start(bf16[16,48,128]{2,1,0:T(8,128)(2,1)} %shard_map.77), calls=%async_computation | async-start | bytes 393216 | tf_op jit(solution)/shard_map/all_to_all | solution.py:305
  9.7 2.1 %shard_map.79 = (f32[48,128]{1,0:T(8,128)S(1)}, bf16[16,8,128]{2,1,0:T(8,128)(2,1)S(1)}, f32[48,128]{1,0:T(8,128)S(1)}, f32[48,128]{1,0:T(8,128)S(1)}) custom-call(f32[11,64,128]{2,1,0:T(8,128)} %bitcast.9, f32[11,64,128]{2,1,0:T(8,128)} %bitcast.10, f32[64,64]{1,0:T(8,128)} %refs_2_.1, f32[64,64]{1,0:T(8,128)} %refs_3_.1, f32[64,64]{1,0:T(8,128)} %refs_4_.1), custom_call_target="tpu_custom_call" | custom-call | tf_op jit(solution)/shard_map/pallas_call | solution.py:323
  11.8 6.1 %all-to-all-done.blocks_ref = bf16[16,48,128]{2,1,0:T(8,128)(2,1)S(1)} async-done(((bf16[16,48,128]{2,1,0:T(8,128)(2,1)}), bf16[16,48,128]{2,1,0:T(8,128)(2,1)S(1)}, u32[]{:S(2)}, u32[]{:S(2)}) %all-to-all-start) | async-done | bytes 196640 | tf_op jit(solution)/shard_map/all_to_all | solution.py:305
  17.9 0.0 copy-start
  17.9 0.1 shard_map.78
  17.9 13.9 %all_to_all.45.pieces_ref = bf16[32,48,128]{2,1,0:T(8,128)(2,1)S(1)} all-to-all(bf16[32,48,128]{2,1,0:T(8,128)(2,1)S(1)} %shard_map.78), channel_id=1, replica_groups=mesh['hist'=16,'rows_0'=4,'rows_1'=4,'rows_2'=2] {'rows_0','rows_1','row..., dimensions={0} | all-to-all | bytes 786432 | tf_op jit(solution)/shard_map/all_to_all | solution.py:305
  31.8 0.0 copy-done
  31.8 0.9 shard_map.80
  32.8 12.0 %all_to_all.46 = bf16[16,56,128]{2,1,0:T(8,128)(2,1)S(1)} all-to-all(bf16[16,56,128]{2,1,0:T(8,128)(2,1)S(1)} %shard_map.80), channel_id=1, replica_groups=mesh['hist'=16,'rows_0'=4,'rows_1'=4,'rows_2'=2] {'rows_0','rows_1'}, dimensions={0} | all-to-all | bytes 458752 | tf_op jit(solution)/shard_map/all_to_all | solution.py:305
  44.8 31.7 %all_to_all.47.arrived_ref = bf16[16,56,128]{2,1,0:T(8,128)(2,1)S(1)} all-to-all(bf16[16,56,128]{2,1,0:T(8,128)(2,1)S(1)} %all_to_all.46), channel_id=1, replica_groups=mesh['hist'=16,'rows_0'=4,'rows_1'=4,'rows_2'=2] {'hist'}, dimensions={0} | all-to-all | bytes 458752 | tf_op jit(solution)/shard_map/all_to_all | solution.py:305
  76.5 0.3 shard_map.81
  76.8 0.1 broadcast_in_dim.4
  76.8 13.8 %all_to_all.48.pieces_ref = bf16[32,48,128]{2,1,0:T(8,128)(2,1)S(1)} all-to-all(bf16[32,48,128]{2,1,0:T(8,128)(2,1)S(1)} %broadcast_in_dim.4), channel_id=1, replica_groups=mesh['hist'=16,'rows_0'=4,'rows_1'=4,'rows_2'=2] {'rows_0','rows_1','row..., dimensions={0} | all-to-all | bytes 786432 | tf_op jit(solution)/shard_map/all_to_all | solution.py:305
  90.6 0.9 shard_map.82
  91.6 11.7 %all_to_all.49 = bf16[16,48,128]{2,1,0:T(8,128)(2,1)S(1)} all-to-all(bf16[16,48,128]{2,1,0:T(8,128)(2,1)S(1)} %shard_map.82), channel_id=1, replica_groups=mesh['hist'=16,'rows_0'=4,'rows_1'=4,'rows_2'=2] {'rows_0','rows_1'}, dimensions={0} | all-to-all | bytes 393216 | tf_op jit(solution)/shard_map/all_to_all | solution.py:305
  103.2 20.5 %all_to_all.50.arrived_ref = bf16[16,48,128]{2,1,0:T(8,128)(2,1)S(1)} all-to-all(bf16[16,48,128]{2,1,0:T(8,128)(2,1)S(1)} %all_to_all.49), channel_id=1, replica_groups=mesh['hist'=16,'rows_0'=4,'rows_1'=4,'rows_2'=2] {'hist'}, dimensions={0} | all-to-all | bytes 393216 | tf_op jit(solution)/shard_map/all_to_all | solution.py:305
  123.8 0.3 shard_map.83
  124.1 0.1 broadcast_in_dim.5
  124.2 14.2 %all_to_all.51.pieces_ref = bf16[32,48,128]{2,1,0:T(8,128)(2,1)S(1)} all-to-all(bf16[32,48,128]{2,1,0:T(8,128)(2,1)S(1)} %broadcast_in_dim.5), channel_id=1, replica_groups=mesh['hist'=16,'rows_0'=4,'rows_1'=4,'rows_2'=2] {'rows_0','rows_1','row..., dimensions={0} | all-to-all | bytes 786432 | tf_op jit(solution)/shard_map/all_to_all | solution.py:305
  138.3 0.9 shard_map.84
  139.3 21.1 %all_to_all.52.arrived_ref = bf16[16,48,128]{2,1,0:T(8,128)(2,1)S(1)} all-to-all(bf16[16,48,128]{2,1,0:T(8,128)(2,1)S(1)} %shard_map.84), channel_id=1, replica_groups=mesh['hist'=16,'rows_0'=4,'rows_1'=4,'rows_2'=2] {'hist'}, dimensions={0} | all-to-all | bytes 393216 | tf_op jit(solution)/shard_map/all_to_all | solution.py:305
  160.4 0.7 shard_map.85
Async XLA Ops:
  2.6 15.2 %all-to-all-start = ((bf16[16,48,128]{2,1,0:T(8,128)(2,1)}), bf16[16,48,128]{2,1,0:T(8,128)(2,1)S(1)}, u32[]{:S(2)}, u32[]{:S(2)}) async-start(bf16[16,48,128]{2,1,0:T(8,128)(2,1)} %shard_map.77), calls=%async_computation | async-start | bytes 393216 | tf_op jit(solution)/shard_map/all_to_all | solution.py:305
  17.9 14.0 %copy-start = (bf16[22,64,11,128]{3,1,2,0:T(8,128)(2,1)S(1)}, bf16[22,64,11,128]{3,1,2,0:T(8,128)(2,1)}, u32[]{:S(2)}) copy-start(bf16[22,64,11,128]{3,1,2,0:T(8,128)(2,1)} %param.6) | copy-start | bytes 11894788
